TPU v7x, 32 devices: a whole 2x2x4 slice. The times are simulated.
32 devices in a mesh: groups: 2 (over x), row: 16 (over z, y, core).
Axes of the slice: x: 2, y: 2, z: 4, core: 2. Of those that a mesh axis runs over, the one named last changes fastest.
Arguments:
- features: bfloat16 [128, 64, 512], P(('groups', 'row')), parts along dimension 0, may hold values from -6 to 6
- cotangent: bfloat16 [128, 64, 512], P(('groups', 'row')), parts along dimension 0, may hold values from -6 to 6
- depth_weight: bfloat16 [49, 512], P(None, 'row'), may hold values from -0.875 to 0.875
- depth_bias: bfloat16 [512], P('row'), may hold values from -3 to 3
- norm_gain: bfloat16 [512], P('row'), may hold values from 0.25 to 1.75
- norm_shift: bfloat16 [512], P('row'), may hold values from -3 to 3
- up_weight: bfloat16 [512, 2048], P('row'), may hold values from -0.25 to 0.25
- up_bias: bfloat16 [2048], P('row'), may hold values from -3 to 3
- down_weight: bfloat16 [2048, 512], P('row'), may hold values from -0.125 to 0.125
- down_bias: bfloat16 [512], P('row'), may hold values from -3 to 3
Outputs:
- block_out: bfloat16 [128, 64, 512], P(('groups', 'row')), parts along dimension 0
- grad_features: bfloat16 [128, 64, 512], P(('groups', 'row')), parts along dimension 0
- grad_up_weight: float32 [1024, 2048], P(('groups', 'row')), parts along dimension 0
- grad_down_weight: float32 [4096, 512], P(('groups', 'row')), parts along dimension 0
- grad_depth_weight: float32 [98, 512], P('groups', 'row'), parts along dimension 0
- grad_depth_bias: float32 [1024], P(('groups', 'row')), parts along dimension 0
- grad_norm_gain: float32 [1024], P(('groups', 'row')), parts along dimension 0
- grad_norm_shift: float32 [1024], P(('groups', 'row')), parts along dimension 0
- grad_up_bias: float32 [4096], P(('groups', 'row')), parts along dimension 0
- grad_down_bias: float32 [1024], P(('groups', 'row')), parts along dimension 0
There are 2 independent parts, one for each index of `groups`. A program takes and returns all parts, laid end to end along the dimension named above; an argument that names none is the same for every part. Nothing has to cross between parts.
All inputs are finite; a program needn't handle non-finite values.
Results may differ from a plain program's by a relative error of at most 0.0055.
Values may be sent and summed in bfloat16 or wider, within the bound.
A program may use at most 64 MiB of HBM per device.

v0:
```python
import math

import jax
import jax.numpy as jnp
from jax import lax
from jax.sharding import PartitionSpec as P

eps = 1e-06


def with_halo(block, sides, width):
    for axis, dim in sides:
        count = lax.axis_size(axis)
        forward = [(i, i + 1) for i in range(count - 1)]
        backward = [(target, source) for source, target in forward]
        low = lax.ppermute(
            lax.slice_in_dim(block, block.shape[dim] - width, None, axis=dim), axis, forward
        )
        high = lax.ppermute(lax.slice_in_dim(block, 0, width, axis=dim), axis, backward)
        block = jnp.concatenate([low, block, high], axis=dim)
    return block


def gelu_value(value):
    return 0.5 * value * (1.0 + lax.erf(value * (1.0 / math.sqrt(2.0))))


def gelu_slope(value):
    cumulative = 0.5 * (1.0 + lax.erf(value * (1.0 / math.sqrt(2.0))))
    density = jnp.exp(-0.5 * value * value) * (1.0 / math.sqrt(2.0 * math.pi))
    return cumulative + value * density


def depth_conv(padded, kernel, height, width):
    total = jnp.zeros((height, width, kernel.shape[1]), jnp.float32)
    for first in range(7):
        for second in range(7):
            total = (
                total
                + padded[first : first + height, second : second + width, :]
                * kernel[first * 7 + second]
            )
    return total


def depth_conv_back(padded, kernel, height, width):
    total = jnp.zeros((height, width, kernel.shape[1]), jnp.float32)
    for first in range(7):
        for second in range(7):
            total = (
                total
                + padded[6 - first : 6 - first + height, 6 - second : 6 - second + width, :]
                * kernel[first * 7 + second]
            )
    return total


def per_device(
    features,
    cotangent,
    depth_weight,
    depth_bias,
    norm_gain,
    norm_shift,
    up_weight,
    up_bias,
    down_weight,
    down_bias,
):
    height, width, chans = features.shape
    devices = lax.axis_size("row")
    cells = height * width
    scale = 1.0 / math.sqrt(cells * devices)
    kernel, conv_bias, gain, shift, bias_down, bias_up = (
        lax.all_gather(depth_weight, "row", axis=1, tiled=True),
        lax.all_gather(depth_bias, "row", axis=0, tiled=True),
        lax.all_gather(norm_gain, "row", axis=0, tiled=True),
        lax.all_gather(norm_shift, "row", axis=0, tiled=True),
        lax.all_gather(down_bias, "row", axis=0, tiled=True),
        lax.all_gather(up_bias, "row", axis=0, tiled=True),
    )
    kernel = kernel.astype(jnp.float32)
    gain = gain.astype(jnp.float32)
    rimmed = with_halo(features, (("row", 0),), 3)
    padded = jnp.pad(rimmed.astype(jnp.float32), ((0, 0), (3, 3), (0, 0)))
    conv = depth_conv(padded, kernel, height, width) + conv_bias.astype(jnp.float32)
    mean_val = jnp.mean(conv, axis=2, keepdims=True)
    centered = conv - mean_val
    var_val = jnp.mean(centered * centered, axis=2, keepdims=True)
    inv = lax.rsqrt(var_val + eps)
    normed = centered * inv
    normal_out = (normed * gain + shift.astype(jnp.float32)).astype(jnp.bfloat16)
    flat_norm = normal_out.reshape(cells, chans)
    flat_cot = cotangent.reshape(cells, chans)
    columns = flat_norm
    hidden = jnp.dot(
        columns,
        lax.all_gather(up_weight, "row", axis=0, tiled=True),
        preferred_element_type=jnp.float32,
    ) + bias_up.astype(jnp.float32)
    act = gelu_value(hidden).astype(jnp.bfloat16)
    columns = act
    mixed = jnp.dot(
        columns,
        lax.all_gather(down_weight, "row", axis=0, tiled=True),
        preferred_element_type=jnp.float32,
    )
    block_out = (
        features.astype(jnp.float32)
        + (mixed + bias_down.astype(jnp.float32)).reshape(height, width, chans)
    ).astype(jnp.bfloat16)
    down_full = (
        lax.dot_general(act, flat_cot, (((0,), (0,)), ((), ())), preferred_element_type=jnp.float32)
        * scale
    )
    grad_down_weight = lax.psum_scatter(down_full, "row", scatter_dimension=0, tiled=True)
    dact = lax.dot_general(
        flat_cot,
        lax.all_gather(down_weight, "row", axis=0, tiled=True),
        (((1,), (1,)), ((), ())),
        preferred_element_type=jnp.float32,
    )
    dhidden = (dact * gelu_slope(hidden)).astype(jnp.bfloat16)
    columns = flat_norm
    grad_up_weight = lax.psum_scatter(
        lax.dot_general(
            columns, dhidden, (((0,), (0,)), ((), ())), preferred_element_type=jnp.float32
        )
        * scale,
        "row",
        scatter_dimension=0,
        tiled=True,
    )
    dnorm = lax.dot_general(
        dhidden,
        lax.all_gather(up_weight, "row", axis=0, tiled=True),
        (((1,), (1,)), ((), ())),
        preferred_element_type=jnp.float32,
    )
    dnorm = dnorm.reshape(height, width, chans)
    down_bias_term = jnp.sum(flat_cot.astype(jnp.float32), axis=0) * scale
    up_bias_term = jnp.sum(dhidden.astype(jnp.float32), axis=0) * scale
    gain_term = jnp.sum(dnorm * normed, axis=(0, 1)) * scale
    shift_term = jnp.sum(dnorm, axis=(0, 1)) * scale
    grad_down_bias, grad_up_bias, grad_norm_gain, grad_norm_shift = (
        lax.psum_scatter(down_bias_term, "row", scatter_dimension=0, tiled=True),
        lax.psum_scatter(up_bias_term, "row", scatter_dimension=0, tiled=True),
        lax.psum_scatter(gain_term, "row", scatter_dimension=0, tiled=True),
        lax.psum_scatter(shift_term, "row", scatter_dimension=0, tiled=True),
    )
    scaled = dnorm * gain
    dconv = inv * (
        scaled
        - jnp.mean(scaled, axis=2, keepdims=True)
        - normed * jnp.mean(scaled * normed, axis=2, keepdims=True)
    )
    dconv = dconv.astype(jnp.bfloat16)
    dconv_wide = dconv.astype(jnp.float32)
    back_rim = with_halo(dconv, (("row", 0),), 3)
    back_pad = jnp.pad(back_rim.astype(jnp.float32), ((0, 0), (3, 3), (0, 0)))
    grad_features = (
        cotangent.astype(jnp.float32) + depth_conv_back(back_pad, kernel, height, width)
    ).astype(jnp.bfloat16)
    taps = []
    for first in range(7):
        for second in range(7):
            taps.append(
                jnp.sum(
                    dconv_wide * padded[first : first + height, second : second + width, :],
                    axis=(0, 1),
                )
            )
    kernel_term = jnp.stack(taps, axis=0) * scale
    conv_bias_term = jnp.sum(dconv_wide, axis=(0, 1)) * scale
    grad_depth_weight, grad_depth_bias = (
        lax.psum_scatter(kernel_term, "row", scatter_dimension=1, tiled=True),
        lax.psum_scatter(conv_bias_term, "row", scatter_dimension=0, tiled=True),
    )
    return (
        block_out,
        grad_features,
        grad_up_weight,
        grad_down_weight,
        grad_depth_weight,
        grad_depth_bias,
        grad_norm_gain,
        grad_norm_shift,
        grad_up_bias,
        grad_down_bias,
    )


def solution(mesh):
    placed = (
        P(("groups", "row"), None, None),
        P(("groups", "row"), None, None),
        P(None, "row"),
        P("row"),
        P("row"),
        P("row"),
        P("row", None),
        P("row"),
        P("row", None),
        P("row"),
    )
    return jax.shard_map(
        per_device,
        mesh=mesh,
        in_specs=placed,
        out_specs=(
            P(("groups", "row"), None, None),
            P(("groups", "row"), None, None),
            P(("groups", "row"), None),
            P(("groups", "row"), None),
            P("groups", "row"),
            P(("groups", "row")),
            P(("groups", "row")),
            P(("groups", "row")),
            P(("groups", "row")),
            P(("groups", "row")),
        ),
        check_vma=False,
    )
```

profile of v0, /device:TPU:0, one launch (start us, length us, event | category | flops | bytes accessed | tf_op | source)
XLA Modules:
  0.0 336.8 jit_solution(5923359344454385601)
XLA Ops:
  7.2 0.0 all-gather.4.cloned.1.call-start
  7.2 0.7 all-gather.4.cloned.1.call-update
  7.9 0.0 all-gather.6.cloned.1.call-start
  8.0 0.7 all-gather.6.cloned.1.call-update
  8.7 0.0 reduce-scatter.10.cloned.1.call-start
  8.7 1.1 fusion.148
  9.8 2.4 collective-permute-start
  12.2 1.3 collective-permute-start.1
  13.5 25.6 %all_gather.26 = bf16[49,512]{0,1:T(8,128)(2,1)S(1)} all-gather(bf16[49,32]{0,1:T(8,128)(2,1)} %param.12), channel_id=1, replica_groups=mesh['groups'=2,'row'=16] {'row'}, dimensions={1}, use_global_device_ids=true | all-gather | bytes 53312 | tf_op jit(solution)/shard_map/all_gather | solution.py:75
  39.1 2.6 slice_reduce_fusion.48
  41.8 0.0 copy-start.62
  41.8 0.0 copy-start.68
  41.8 0.0 copy-start.69
  41.8 1.6 slice_reduce_fusion.46
  43.5 0.6 fusion.149
  44.7 0.2 dynamic-update-slice
  45.0 0.2 dynamic-update-slice.1
  45.2 0.2 dynamic-update-slice.2
  45.5 0.2 dynamic-update-slice.3
  45.7 30.5 %all-reduce.12 = (bf16[512]{0:T(512)(128)(2,1)S(1)}, bf16[512]{0:T(512)(128)(2,1)S(1)}, bf16[512]{0:T(512)(128)(2,1)S(1)}, bf16[512]{0:T(512)(128)(2,1)}) all-reduce(bf16[512]{0:T(512)(128)(2,1)S(1)} %dynamic-update-slice, bf16[512]{0:T(512)(128)(2,1)S(1)} %dynamic-update-slice.2, ...), channel_id=1, replica_groups=mesh['groups'=2,'row'=16] {'row'}, use_global_device_ids=true, to_apply=%add.2 | all-reduce | flops 2048 | bytes 8192
  76.2 17.5 %all-gather = bf16[16,1,128]{2,1,0:T(2,128)(2,1)S(1)} all-gather(bf16[1,1,128]{2,1,0:T(2,128)(2,1)S(1)} %bitcast.131), channel_id=1, replica_groups=mesh['groups'=2,'row'=16] {'row'}, dimensions={0}, use_global_device_ids=true | all-gather | bytes 4352 | tf_op jit(solution)/shard_map/all_gather | solution.py:80
  93.8 2.7 slice_reduce_fusion.47
  96.7 0.1 maximum_convert_fusion
  96.8 4.7 %fusion.146 = (f32[4,64]{1,0:T(4,128)S(1)}, f32[4,64,512]{2,1,0:T(8,128)S(1)}) fusion(f32[512]{0:T(512)S(1)} %convert_element_type.62, f32[512]{0:T(512)S(1)} %get-tuple-element.85, f32[512]{0:T(512)S(1)} %get-tuple-element.86, f32[512]{0:T(512)S(1)} %get-tuple-element.87, f32[512]{0:T(512)S(1)} %get-tuple-element.88, ...), kind=kLoop, calls=%fused_computation.368 | loop fusion | flops 12975872 | bytes 5608448 | tf_op jit(solution)/shard_map/reduce_sum | solution.py:87
  101.7 0.2 multiply_reduce_fusion.3
  101.9 0.2 add_convert_fusion.1
  102.1 0.0 copy-start.2
  102.1 0.0 all-gather.4.cloned.1.call-done
  102.1 3.8 %multiply_convert_fusion = (bf16[256,2048]{1,0:T(8,128)(2,1)S(1)}, f32[256,2048]{1,0:T(8,128)}) fusion(f32[2048]{0:T(1024)S(1)} %bitcast.81, bf16[256,512]{1,0:T(8,128)(2,1)S(1)} %bitcast.75, bf16[512,2048]{1,0:T(8,128)(2,1)} %all-gather.4.cloned.1.call-done), kind=kOutput, calls=%fused_computation.61 | convolution fusion | flops 540016640 | bytes 5513216 | tf_op jit(solution)/shard_map/dot_general | solution.py:96
  106.0 4.2 %convert_reduce_fusion.1 = (f32[2048]{0:T(1024)}, bf16[256,2048]{1,0:T(8,128)(2,1)S(1)}) fusion(f32[256,2048]{1,0:T(8,128)} %get-tuple-element.152, bf16[256,512]{1,0:T(8,128)(2,1)} %bitcast.77, bf16[2048,512]{1,0:T(8,128)(2,1)} %all-gather.6.cloned.1.call-done), kind=kOutput, calls=%fused_computation.60 | convolution fusion | flops 543160320 | bytes 5513216 | tf_op jit(solution)/shard_map/dot_general | solution.py:117
  110.2 1.3 fusion.145
  111.5 0.8 copy-done
  112.3 0.8 multiply_reduce_fusion
  113.1 0.6 broadcast_multiply_fusion.6
  113.7 0.7 div.17
  114.4 3.2 fusion.143
  117.5 1.4 fusion.142
  119.1 0.0 copy-start.3
  119.1 1.0 fusion.144
  120.3 2.3 stack.199
  122.6 0.9 copy.22
  123.5 0.0 reduce-scatter.10.cloned.1.call-update
  123.5 0.3 reduce-scatter.6.cloned.1.call-start
  123.8 3.9 %convolution_multiply_fusion.1 = f32[512,2048]{1,0:T(8,128)} fusion(bf16[256,512]{1,0:T(8,128)(2,1)S(1)} %bitcast.76, bf16[256,2048]{1,0:T(8,128)(2,1)} %copy-done.6), kind=kOutput, calls=%fused_computation.51 | convolution fusion | flops 537919488 | bytes 5505024 | tf_op jit(solution)/shard_map/dot_general | solution.py:126
  127.7 0.0 reduce-scatter.6.cloned.1.call-update
  127.7 0.0 reduce-scatter.8.cloned.1.call-start
  127.7 0.9 copy-done.4
  128.6 2.7 convolution_multiply_fusion
  131.3 0.0 reduce-scatter.8.cloned.1.call-update
  132.7 0.1 convert_reduce_fusion.2
  132.8 59.3 %all-reduce.11 = (f32[512]{0:T(512)S(1)}, f32[512]{0:T(512)S(1)}, f32[512]{0:T(512)S(1)}, f32[2048]{0:T(1024)S(1)}, f32[512]{0:T(512)S(1)}) all-reduce(f32[512]{0:T(512)S(1)} %broadcast_multiply_fusion.5, f32[512]{0:T(512)S(1)} %get-tuple-element.157, ...), channel_id=5, replica_groups=mesh['groups'=2,'row'=16] {'row'}, use_global_device_ids=true, to_apply=%region_57.58.clone | all-reduce | flops 4096 | bytes 32768
  192.1 0.6 dynamic-slice.13
  192.7 0.6 dynamic-slice.9
  193.3 0.6 dynamic-slice.7
  193.9 0.6 dynamic-slice.5
  194.5 1.3 collective-permute-start.2
  195.8 1.3 collective-permute-start.3
  197.1 0.6 dynamic-slice.11
  197.7 2.4 convolution_add_fusion.1
  200.3 0.8 add_convert_fusion
  201.1 0.1 maximum_convert_fusion.1
  201.4 4.7 %fusion.5 = bf16[4,64,512]{2,1,0:T(8,128)(2,1)} fusion(bf16[4,64,512]{2,1,0:T(8,128)(2,1)S(1)} %copy-done.4, f32[10,64,512]{2,1,0:T(8,128)S(1)} %maximum_convert_fusion.1, f32[512]{0:T(512)S(1)} %get-tuple-element.85, f32[512]{0:T(512)S(1)} %get-tuple-element.86, f32[512]{0:T(512)S(1)} %get-tuple-element.87, f32[512]{0:T(512)S(1)} %get-tuple-element.88, ...), kind=kLoop, calls=%fused_computation.152 | loop fusion | flops 13107200 | bytes 5605376 | tf_op jit(solution)/shard_map/convert_element_type | solution.py:163
  206.0 48.2 %reduce-scatter.6.cloned.1.call-done = f32[32,2048]{1,0:T(8,128)} async-done(((f32[512,2048]{1,0:T(8,128)}), f32[32,2048]{1,0:T(8,128)}) %reduce-scatter.6.cloned.1.call-update) | async-done | bytes 262160 | tf_op jit(solution)/shard_map/reduce_scatter | solution.py:125
  254.2 76.1 %reduce-scatter.8.cloned.1.call-done = f32[128,512]{1,0:T(8,128)} async-done(((f32[2048,512]{1,0:T(8,128)}), f32[128,512]{1,0:T(8,128)}) %reduce-scatter.8.cloned.1.call-update) | async-done | bytes 262160 | tf_op jit(solution)/shard_map/reduce_scatter | solution.py:116
  (158 shorter events, 0.4 us)
Async XLA Ops:
  7.2 94.9 %all-gather.4.cloned.1.call-start = ((), (), s32[]{:S(2)}) async-start(), calls=%async_computation.3 | async-start | bytes 2228224 | tf_op jit(solution)/shard_map/all_gather | solution.py:98
  7.9 98.0 %all-gather.6.cloned.1.call-start = ((), (), s32[]{:S(2)}) async-start(), calls=%async_computation.4 | async-start | bytes 2228224 | tf_op jit(solution)/shard_map/all_gather | solution.py:105
  8.7 197.4 %reduce-scatter.10.cloned.1.call-start = ((), (), s32[]{:S(2)}) async-start(), calls=%async_computation.7 | async-start | bytes 278528
  9.8 86.9 %collective-permute-start = (bf16[3,64,512]{2,1,0:T(8,128)(2,1)S(1)}, bf16[3,64,512]{2,1,0:T(8,128)(2,1)S(1)}, u32[]{:S(2)}, u32[]{:S(2)}) collective-permute-start(bf16[3,64,512]{2,1,0:T(8,128)(2,1)S(1)} %get-tuple-element.147), channel_id=1, source_target_pairs={{0,1},{1,2},{2,3},{3,4},{4,5},{5,6},{6,7},{7,8},{8,9},{9,10},{10,1... | collective-permute-start | bytes 589832 | tf_op jit(solution)/shard_map/ppermute | solution.py:16
  12.2 84.5 %collective-permute-start.1 = (bf16[3,64,512]{2,1,0:T(8,128)(2,1)S(1)}, bf16[3,64,512]{2,1,0:T(8,128)(2,1)S(1)}, u32[]{:S(2)}, u32[]{:S(2)}) collective-permute-start(bf16[3,64,512]{2,1,0:T(8,128)(2,1)S(1)} %get-tuple-element.148), channel_id=1, source_target_pairs={{1,0},{2,1},{3,2},{4,3},{5,4},{6,5},{7,6},{8,7},{9,8},{10,9},{11,1... | collective-permute-start | bytes 589832 | tf_op jit(solution)/shard_map/ppermute | solution.py:19
  41.8 1.7 copy-start.62
  41.8 2.9 copy-start.66
  41.8 3.2 copy-start.67
  41.8 3.4 %copy-start.68 = (bf16[32]{0:T(256)(128)(2,1)S(1)}, bf16[32]{0:T(256)(128)(2,1)}, u32[]{:S(2)}) copy-start(bf16[32]{0:T(256)(128)(2,1)} %param.15) | copy-start | bytes 196
  41.8 3.7 %copy-start.69 = (bf16[32]{0:T(256)(128)(2,1)S(1)}, bf16[32]{0:T(256)(128)(2,1)}, u32[]{:S(2)}) copy-start(bf16[32]{0:T(256)(128)(2,1)} %param.19) | copy-start | bytes 196
  41.8 34.4 %copy-start.65 = (bf16[128]{0:T(256)(128)(2,1)S(1)}, bf16[128]{0:T(256)(128)(2,1)}, u32[]{:S(2)}) copy-start(bf16[128]{0:T(256)(128)(2,1)} %param.17) | copy-start | bytes 772
  93.8 2.9 copy-start.1
  96.5 5.0 %copy-start.7 = (f32[512]{0:T(512)}, f32[512]{0:T(512)S(1)}, u32[]{:S(2)}) copy-start(f32[512]{0:T(512)S(1)} %get-tuple-element.104) | copy-start | bytes 6148
  96.5 5.0 %copy-start.9 = (f32[512]{0:T(512)}, f32[512]{0:T(512)S(1)}, u32[]{:S(2)}) copy-start(f32[512]{0:T(512)S(1)} %get-tuple-element.105) | copy-start | bytes 6148
  96.5 5.0 %copy-start.11 = (f32[512]{0:T(512)}, f32[512]{0:T(512)S(1)}, u32[]{:S(2)}) copy-start(f32[512]{0:T(512)S(1)} %get-tuple-element.106) | copy-start | bytes 6148
  96.5 5.0 %copy-start.13 = (f32[512]{0:T(512)}, f32[512]{0:T(512)S(1)}, u32[]{:S(2)}) copy-start(f32[512]{0:T(512)S(1)} %get-tuple-element.107) | copy-start | bytes 6148
  96.5 5.0 %copy-start.15 = (f32[512]{0:T(512)}, f32[512]{0:T(512)S(1)}, u32[]{:S(2)}) copy-start(f32[512]{0:T(512)S(1)} %get-tuple-element.108) | copy-start | bytes 6148
  96.5 5.0 %copy-start.17 = (f32[512]{0:T(512)}, f32[512]{0:T(512)S(1)}, u32[]{:S(2)}) copy-start(f32[512]{0:T(512)S(1)} %get-tuple-element.109) | copy-start | bytes 6148
  96.5 5.0 %copy-start.19 = (f32[512]{0:T(512)}, f32[512]{0:T(512)S(1)}, u32[]{:S(2)}) copy-start(f32[512]{0:T(512)S(1)} %get-tuple-element.110) | copy-start | bytes 6148
  96.5 5.0 %copy-start.21 = (f32[512]{0:T(512)}, f32[512]{0:T(512)S(1)}, u32[]{:S(2)}) copy-start(f32[512]{0:T(512)S(1)} %get-tuple-element.111) | copy-start | bytes 6148
  96.6 5.0 %copy-start.23 = (f32[512]{0:T(512)}, f32[512]{0:T(512)S(1)}, u32[]{:S(2)}) copy-start(f32[512]{0:T(512)S(1)} %get-tuple-element.112) | copy-start | bytes 6148
  96.6 5.0 %copy-start.25 = (f32[512]{0:T(512)}, f32[512]{0:T(512)S(1)}, u32[]{:S(2)}) copy-start(f32[512]{0:T(512)S(1)} %get-tuple-element.113) | copy-start | bytes 6148
  96.6 5.0 %copy-start.27 = (f32[512]{0:T(512)}, f32[512]{0:T(512)S(1)}, u32[]{:S(2)}) copy-start(f32[512]{0:T(512)S(1)} %get-tuple-element.114) | copy-start | bytes 6148
  96.6 5.0 %copy-start.29 = (f32[512]{0:T(512)}, f32[512]{0:T(512)S(1)}, u32[]{:S(2)}) copy-start(f32[512]{0:T(512)S(1)} %get-tuple-element.115) | copy-start | bytes 6148
  96.6 5.0 %copy-start.31 = (f32[512]{0:T(512)}, f32[512]{0:T(512)S(1)}, u32[]{:S(2)}) copy-start(f32[512]{0:T(512)S(1)} %get-tuple-element.116) | copy-start | bytes 6148
  96.6 5.0 %copy-start.33 = (f32[512]{0:T(512)}, f32[512]{0:T(512)S(1)}, u32[]{:S(2)}) copy-start(f32[512]{0:T(512)S(1)} %get-tuple-element.117) | copy-start | bytes 6148
  96.6 5.0 %copy-start.35 = (f32[512]{0:T(512)}, f32[512]{0:T(512)S(1)}, u32[]{:S(2)}) copy-start(f32[512]{0:T(512)S(1)} %get-tuple-element.118) | copy-start | bytes 6148
  96.6 5.0 %copy-start.37 = (f32[512]{0:T(512)}, f32[512]{0:T(512)S(1)}, u32[]{:S(2)}) copy-start(f32[512]{0:T(512)S(1)} %get-tuple-element.119) | copy-start | bytes 6148
  96.6 5.0 %copy-start.39 = (f32[512]{0:T(512)}, f32[512]{0:T(512)S(1)}, u32[]{:S(2)}) copy-start(f32[512]{0:T(512)S(1)} %get-tuple-element.120) | copy-start | bytes 6148
  96.7 5.0 %copy-start.41 = (f32[512]{0:T(512)}, f32[512]{0:T(512)S(1)}, u32[]{:S(2)}) copy-start(f32[512]{0:T(512)S(1)} %get-tuple-element.121) | copy-start | bytes 6148
  102.1 3.9 %copy-start.2 = (bf16[4,64,512]{2,1,0:T(8,128)(2,1)}, bf16[4,64,512]{2,1,0:T(8,128)(2,1)S(1)}, u32[]{:S(2)}) copy-start(bf16[4,64,512]{2,1,0:T(8,128)(2,1)S(1)} %add_convert_fusion.1) | copy-start | bytes 786436
  106.0 4.2 %copy-start.5 = (bf16[512,2048]{1,0:T(8,128)(2,1)S(1)}, bf16[512,2048]{1,0:T(8,128)(2,1)}, u32[]{:S(2)}) copy-start(bf16[512,2048]{1,0:T(8,128)(2,1)} %all-gather.4.cloned.1.call-done) | copy-start | bytes 6291460
  110.2 2.9 copy-start.6
  118.9 1.2 copy-start.43
  118.9 1.2 copy-start.44
  119.0 1.2 copy-start.45
  119.0 1.2 copy-start.46
  119.0 1.2 copy-start.47
  119.0 1.2 copy-start.48
  119.0 1.2 copy-start.49
  119.0 1.2 copy-start.50
  119.0 1.2 copy-start.51
  119.0 1.2 copy-start.52
  119.0 1.2 copy-start.53
  119.0 1.2 copy-start.54
  119.0 1.2 copy-start.55
  119.0 1.2 copy-start.56
  119.0 1.2 copy-start.57
  119.1 1.2 copy-start.58
  119.1 4.7 %copy-start.3 = (bf16[4,64,512]{2,1,0:T(8,128)(2,1)S(1)}, bf16[4,64,512]{2,1,0:T(8,128)(2,1)}, u32[]{:S(2)}) copy-start(bf16[4,64,512]{2,1,0:T(8,128)(2,1)} %copy-done.2) | copy-start | bytes 786436
  123.5 130.7 %reduce-scatter.6.cloned.1.call-start = ((), (), s32[]{:S(2)}) async-start(), calls=%async_computation.5 | async-start | bytes 4456448 | tf_op jit(solution)/shard_map/reduce_scatter | solution.py:125
  127.7 202.6 %reduce-scatter.8.cloned.1.call-start = ((), (), s32[]{:S(2)}) async-start(), calls=%async_computation.6 | async-start | bytes 4456448 | tf_op jit(solution)/shard_map/reduce_scatter | solution.py:116
  131.3 1.3 copy-start.64
  131.3 1.4 copy-start.61
  131.3 1.5 copy-start.59
  131.3 1.5 copy-start.63
  131.3 1.5 copy-start.60
  194.5 6.6 %collective-permute-start.2 = (bf16[3,64,512]{2,1,0:T(8,128)(2,1)S(1)}, bf16[3,64,512]{2,1,0:T(8,128)(2,1)S(1)}, u32[]{:S(2)}, u32[]{:S(2)}) collective-permute-start(bf16[3,64,512]{2,1,0:T(8,128)(2,1)S(1)} %get-tuple-element.145), channel_id=1, source_target_pairs={{0,1},{1,2},{2,3},{3,4},{4,5},{5,6},{6,7},{7,8},{8,9},{9,10},{10,1... | collective-permute-start | bytes 589832 | tf_op jit(solution)/shard_map/ppermute | solution.py:16
  195.8 5.3 %collective-permute-start.3 = (bf16[3,64,512]{2,1,0:T(8,128)(2,1)S(1)}, bf16[3,64,512]{2,1,0:T(8,128)(2,1)S(1)}, u32[]{:S(2)}, u32[]{:S(2)}) collective-permute-start(bf16[3,64,512]{2,1,0:T(8,128)(2,1)S(1)} %get-tuple-element.146), channel_id=1, source_target_pairs={{1,0},{2,1},{3,2},{4,3},{5,4},{6,5},{7,6},{8,7},{9,8},{10,9},{11,1... | collective-permute-start | bytes 589832 | tf_op jit(solution)/shard_map/ppermute | solution.py:19
  200.1 1.1 copy-start.8
  200.1 1.1 copy-start.10
  200.1 1.1 copy-start.12
  200.1 1.1 copy-start.14
  200.1 1.1 copy-start.16
  (15 other events, 15.6 us)
Sparse Core Ops, SparseCore 0:
  10.1 44.2 all-gather.3
  56.6 40.1 all-gather.5
  123.6 54.3 reduce-scatter.9
  182.2 71.8 reduce-scatter.5
  258.4 71.7 reduce-scatter.7
where the time goes:
time: 337 us
  blocking collectives  133 us (39%)
  waiting for transfers between devices  126 us (37%)
  matrix products  18.4 us (5%)
  local copies, waits for them, and re-layouts  18.3 us (5%)
  other arithmetic  17.8 us (5%)
  between operations  16.9 us (5%)
  starting transfers between devices  6.71 us (2%)
    unnamed x2, blocking collectives  89.8 us
    reduce_scatter x1, waiting for transfers between devices, per_device(): lax.psum_scatter(down_full, 'row', scatter_dimension=0, tiled=True)  76.1 us
    reduce_scatter x1, waiting for transfers between devices, per_device(): lax.psum_scatter(lax.dot_general(columns, dhidden, (((0,), (0,)), ((), ()...  48.2 us
    all_gather x1, blocking collectives, per_device(): lax.all_gather(depth_weight, 'row', axis=1, tiled=True)  25.6 us
    all_gather x1, blocking collectives, per_device(): lax.all_gather(up_bias, 'row', axis=0, tiled=True)  17.5 us
    unnamed x155, local copies, waits for them, and re-layouts  7.34 us
    slice x3, local copies, waits for them, and re-layouts, depth_conv(): kernel[first * 7 + second]  6.92 us
  transfers between devices with their start and end apart: 9, of which 2 were waited for; matrix products, arithmetic and copies ran while one was open for 11% of the time, Pallas kernels for 0%

commit v1 on v0

v1 whole, which is shorter than its diff:
```python
import functools
import math

import jax
import jax.numpy as jnp
from jax import lax
from jax.experimental import pallas as pl
from jax.experimental.pallas import tpu as pltpu
from jax.sharding import PartitionSpec as P

eps = 1e-06
LANES = 128
HALO = 3


class Ring:
    def __init__(self, devices, fold):
        self.devices, self.fold = devices, fold
        self.chips = devices // 2
        self.length = self.chips // fold
        half = self.chips // 2
        rest = self.chips - 1 - half
        self.flows = [(1, 0, half), (-1, 1, half), (-1, 0, rest), (1, 1, rest)]
        self.most = max(half, 1)

    def place(self, chip):
        major, minor = chip // self.fold, chip % self.fold
        return minor * (2 * self.length - 1) + major * (1 - 2 * minor)

    def chip_at(self, place):
        place = lax.rem(place + 2 * self.chips, self.chips)
        minor = place // self.length
        major = minor * (2 * self.length - 1) + place * (1 - 2 * minor)
        return major * self.fold + minor


def fold_of(mesh):
    line = mesh.devices.reshape(mesh.shape["groups"], mesh.shape["row"])[0]
    spots = [getattr(device, "coords", None) for device in line[::2]]
    if any(spot is None for spot in spots) or len(spots) < 2:
        return 1
    spots = [tuple(spot) for spot in spots]
    varying = [axis for axis in range(3) if len({spot[axis] for spot in spots}) > 1]
    fast = [axis for axis in varying if spots[0][axis] != spots[1][axis]]
    if len(varying) == 2 and len(fast) == 1 and len({spot[fast[0]] for spot in spots}) == 2:
        return 2
    return 1


def greet_all(me, devices):
    barrier = pltpu.get_barrier_semaphore()

    @pl.loop(1, devices)
    def _(step):
        pl.semaphore_signal(barrier, inc=1, device_id={"row": lax.rem(me + step, devices)})

    pl.semaphore_wait(barrier, devices - 1)


def send(src, dst, send_sem, recv_sem, target):
    return pltpu.make_async_remote_copy(
        src_ref=src,
        dst_ref=dst,
        send_sem=send_sem,
        recv_sem=recv_sem,
        device_id={"row": target},
        device_id_type=pl.DeviceIdType.MESH,
    )


def gather_kernel(
    ring, up, down, small, feat,
    all_up, all_down, all_small, rim,
    ring_out, ring_in, pair_out, pair_in, small_out, small_in, rim_out, rim_in, own_sem,
):
    devices = ring.devices
    me = lax.axis_index("row")
    core, chip = me % 2, me // 2
    partner = me + 1 - 2 * core
    place = ring.place(chip)
    mine, gathered = (up, down), (all_up, all_down)
    greet_all(me, devices)
    height = feat.shape[0]

    def lower_rim():
        return send(feat.at[pl.ds(height - HALO, HALO)], rim.at[0], rim_out.at[0], rim_in.at[0], lax.rem(me + 1, devices))

    def upper_rim():
        return send(feat.at[pl.ds(0, HALO)], rim.at[1], rim_out.at[1], rim_in.at[1], lax.rem(me + devices - 1, devices))

    @pl.when(me < devices - 1)
    def _():
        lower_rim().start()

    @pl.when(me > 0)
    def _():
        upper_rim().start()

    def small_copy(step):
        return send(small, all_small.at[me], small_out.at[step], small_in.at[step], lax.rem(me + step, devices))

    def small_arrival(step):
        source = lax.rem(me + devices - step, devices)
        return send(small, all_small.at[source], small_out.at[step], small_in.at[step], source)

    @pl.loop(1, devices)
    def _(step):
        small_copy(step).start()

    def owner(flow, step):
        return ring.chip_at(place - ring.flows[flow][0] * step) * 2 + core

    def hop(flow, step):
        direction, which, _ = ring.flows[flow]
        slot = owner(flow, step - 1)
        src = mine[which] if step == 1 else gathered[which].at[slot]
        target = ring.chip_at(place + direction) * 2 + core
        return send(src, gathered[which].at[slot], ring_out.at[flow, step - 1], ring_in.at[flow, step - 1], target)

    def hop_arrival(flow, step):
        direction, which, _ = ring.flows[flow]
        slot = owner(flow, step)
        source = ring.chip_at(place - direction) * 2 + core
        ref = gathered[which].at[slot]
        return send(ref, ref, ring_out.at[flow, step - 1], ring_in.at[flow, step - 1], source)

    def hand(flow, step):
        which = ring.flows[flow][1]
        slot = me if step == 0 else owner(flow, step)
        src = mine[which] if step == 0 else gathered[which].at[slot]
        return send(src, gathered[which].at[slot], pair_out.at[flow, step], pair_in.at[flow, step], partner)

    def hand_arrival(flow, step):
        which = ring.flows[flow][1]
        slot = (partner if step == 0 else ring.chip_at(place - ring.flows[flow][0] * step) * 2 + 1 - core)
        ref = gathered[which].at[slot]
        return send(ref, ref, pair_out.at[flow, step], pair_in.at[flow, step], partner)

    flows = range(len(ring.flows))
    for step in range(1, ring.most + 1):
        for flow in flows:
            hops = ring.flows[flow][2]
            if step <= hops:
                if step > 1:
                    hop_arrival(flow, step - 1).wait_recv()
                hop(flow, step).start()
                if step > 1:
                    hand(flow, step - 1).start()
        if step == 1:
            for flow in (0, 1):
                hand(flow, 0).start()
            owns = [
                pltpu.make_async_copy(up, all_up.at[me], own_sem.at[0]),
                pltpu.make_async_copy(down, all_down.at[me], own_sem.at[1]),
                pltpu.make_async_copy(small, all_small.at[me], own_sem.at[2]),
            ]
            for own in owns:
                own.start()

            @pl.when(me == 0)
            def _():
                rim[0] = jnp.zeros(rim.shape[1:], rim.dtype)

            @pl.when(me == devices - 1)
            def _():
                rim[1] = jnp.zeros(rim.shape[1:], rim.dtype)

    for flow in flows:
        hops = ring.flows[flow][2]
        hop_arrival(flow, hops).wait_recv()
        hand(flow, hops).start()
    for flow in flows:
        hops = ring.flows[flow][2]
        for step in range(0 if flow < 2 else 1, hops + 1):
            hand_arrival(flow, step).wait_recv()
            hand(flow, step).wait_send()
        for step in range(1, hops + 1):
            hop(flow, step).wait_send()

    @pl.loop(1, devices)
    def _(step):
        small_arrival(step).wait_recv()
        small_copy(step).wait_send()

    for own in owns:
        own.wait()

    @pl.when(me < devices - 1)
    def _():
        lower_rim().wait_send()
        upper_rim().wait_recv()

    @pl.when(me > 0)
    def _():
        upper_rim().wait_send()
        lower_rim().wait_recv()


def scatter_kernel(
    ring, up, down, small,
    own_up, own_down, own_small,
    half_up, half_down, got_up, got_down, out_up, out_down, got_small,
    ring_out, ring_in, pair_out, pair_in, small_out, small_in,
):
    devices = ring.devices
    me = lax.axis_index("row")
    core, chip = me % 2, me // 2
    partner = me + 1 - 2 * core
    place = ring.place(chip)
    parts, halves = (up, down), (half_up, half_down)
    got, out, total = (got_up, got_down), (out_up, out_down), (own_up, own_down)
    greet_all(me, devices)

    def pair(which, offset):
        slot = ring.chip_at(place + offset)
        return send(
            parts[which].at[slot, 1 - core], halves[which].at[offset],
            pair_out.at[which, offset], pair_in.at[which, offset], partner,
        )

    half = ring.chips // 2
    order = [half]
    for near in range(half - 1, 0, -1):
        order += [near, ring.chips - near]
    order.append(0)
    for offset in order:
        for which in (0, 1):
            pair(which, offset).start()

    def small_copy(step):
        target = lax.rem(me + step, devices)
        return send(small.at[target], got_small.at[step], small_out.at[step], small_in.at[step], target)

    @pl.loop(1, devices)
    def _(step):
        small_copy(step).start()

    def hop(flow, step):
        direction, which, _ = ring.flows[flow]
        side = 0 if direction > 0 else 1
        target = ring.chip_at(place + direction) * 2 + core
        return send(
            out[which].at[side, step - 1], got[which].at[side, step - 1],
            ring_out.at[flow, step - 1], ring_in.at[flow, step - 1], target,
        )

    known = set()

    def chip_sum(which, offset):
        offset = offset % ring.chips
        if (which, offset) not in known:
            pair(which, offset).wait_recv()
            known.add((which, offset))
        slot = ring.chip_at(place + offset)
        return parts[which][slot, core].astype(jnp.float32) + halves[which][offset].astype(jnp.float32)

    flows = range(len(ring.flows))
    for step in range(1, ring.most + 1):
        for flow in flows:
            direction, which, hops = ring.flows[flow]
            side = 0 if direction > 0 else 1
            if step <= hops:
                value = chip_sum(which, direction * (hops - step + 1))
                if step > 1:
                    hop(flow, step - 1).wait_recv()
                    value = value + got[which][side, step - 2].astype(jnp.float32)
                out[which][side, step - 1] = value.astype(out[which].dtype)
                hop(flow, step).start()

    step_sum = small[me]
    for step in range(1, devices):
        small_copy(step).wait_recv()
        step_sum = step_sum + got_small[step]
    own_small[...] = step_sum
    for which in (0, 1):
        value = chip_sum(which, 0)
        for flow in flows:
            direction, flow_which, hops = ring.flows[flow]
            side = 0 if direction > 0 else 1
            if flow_which == which:
                hop(flow, hops).wait_recv()
                value = value + got[which][side, hops - 1].astype(jnp.float32)
        total[which][...] = value

    for offset in order:
        for which in (0, 1):
            pair(which, offset).wait_send()
    for flow in flows:
        for step in range(1, ring.flows[flow][2] + 1):
            hop(flow, step).wait_send()

    @pl.loop(1, devices)
    def _(step):
        small_copy(step).wait_send()


def vmem():
    return pl.BlockSpec(memory_space=pltpu.VMEM)


def gather(ring, up, down, small, feat):
    devices, most, flows = ring.devices, ring.most, len(ring.flows)
    dma = pltpu.SemaphoreType.DMA
    return pl.pallas_call(
        functools.partial(gather_kernel, ring),
        out_shape=(
            jax.ShapeDtypeStruct((devices,) + up.shape, up.dtype),
            jax.ShapeDtypeStruct((devices,) + down.shape, down.dtype),
            jax.ShapeDtypeStruct((devices,) + small.shape, small.dtype),
            jax.ShapeDtypeStruct((2, HALO) + feat.shape[1:], feat.dtype),
        ),
        in_specs=[vmem()] * 4,
        out_specs=(vmem(),) * 4,
        scratch_shapes=[
            dma((flows, most)), dma((flows, most)),
            dma((flows, most + 1)), dma((flows, most + 1)),
            dma((devices,)), dma((devices,)),
            dma((2,)), dma((2,)), dma((3,)),
        ],
        compiler_params=pltpu.CompilerParams(
            collective_id=0, has_side_effects=True, vmem_limit_bytes=56 * 2**20
        ),
        name="gather",
    )(up, down, small, feat)


def scatter(ring, up, down, small):
    devices, most, flows, chips = ring.devices, ring.most, len(ring.flows), ring.chips
    dma = pltpu.SemaphoreType.DMA
    block_up, block_down = up.shape[2:], down.shape[2:]
    kind = up.dtype
    return pl.pallas_call(
        functools.partial(scatter_kernel, ring),
        out_shape=(
            jax.ShapeDtypeStruct(block_up, jnp.float32),
            jax.ShapeDtypeStruct(block_down, jnp.float32),
            jax.ShapeDtypeStruct(small.shape[1:], jnp.float32),
        ),
        in_specs=[vmem()] * 3,
        out_specs=(vmem(),) * 3,
        scratch_shapes=[
            pltpu.VMEM((chips,) + block_up, kind),
            pltpu.VMEM((chips,) + block_down, kind),
            pltpu.VMEM((2, most) + block_up, kind),
            pltpu.VMEM((2, most) + block_down, kind),
            pltpu.VMEM((2, most) + block_up, kind),
            pltpu.VMEM((2, most) + block_down, kind),
            pltpu.VMEM(small.shape, jnp.float32),
            dma((flows, most)), dma((flows, most)),
            dma((2, chips)), dma((2, chips)),
            dma((devices,)), dma((devices,)),
        ],
        compiler_params=pltpu.CompilerParams(
            collective_id=1, has_side_effects=True, vmem_limit_bytes=56 * 2**20
        ),
        name="scatter",
    )(up, down, small)


def gelu_parts(value):
    cumulative = 0.5 * (1.0 + lax.erf(value * (1.0 / math.sqrt(2.0))))
    density = jnp.exp(-0.5 * value * value) * (1.0 / math.sqrt(2.0 * math.pi))
    return value * cumulative, cumulative + value * density


def depth_conv(padded, kernel, height, width, flip):
    total = jnp.zeros((height, width, kernel.shape[1]), jnp.float32)
    for first in range(7):
        for second in range(7):
            top, left = (6 - first, 6 - second) if flip else (first, second)
            total = total + padded[top : top + height, left : left + width, :] * kernel[first * 7 + second]
    return total


def per_device(
    ring,
    features,
    cotangent,
    depth_weight,
    depth_bias,
    norm_gain,
    norm_shift,
    up_weight,
    up_bias,
    down_weight,
    down_bias,
):
    height, width, chans = features.shape
    devices = ring.devices
    cells = height * width
    own = chans // devices
    units = up_weight.shape[1]
    ratio = units // chans
    scale = 1.0 / math.sqrt(cells * devices)
    packed = jnp.concatenate(
        [depth_weight, depth_bias[None], norm_gain[None], norm_shift[None], down_bias[None], up_bias.reshape(ratio, own)],
        axis=0,
    )
    rows = packed.shape[0]
    filled = -(-rows // 64) * 64
    packed = jnp.pad(packed, ((0, filled - rows), (0, 0))).reshape(filled * own // LANES, LANES)
    all_up, all_down, all_small, rim = gather(ring, up_weight, down_weight, packed, features)
    up_full = all_up.reshape(chans, units)
    down_full = all_down.reshape(units, chans)
    all_small = all_small.reshape(devices, filled, own).transpose(1, 0, 2)
    wide = all_small.reshape(filled, chans).astype(jnp.float32)
    taps = depth_weight.shape[0]
    kernel, conv_bias, gain, shift, bias_down = wide[:taps], wide[taps], wide[taps + 1], wide[taps + 2], wide[taps + 3]
    bias_up = all_small[taps + 4 : taps + 4 + ratio].transpose(1, 0, 2).reshape(units).astype(jnp.float32)

    rimmed = jnp.concatenate([rim[0], features, rim[1]], axis=0)
    padded = jnp.pad(rimmed.astype(jnp.float32), ((0, 0), (3, 3), (0, 0)))
    conv = depth_conv(padded, kernel, height, width, False) + conv_bias
    mean_val = jnp.mean(conv, axis=2, keepdims=True)
    centered = conv - mean_val
    var_val = jnp.mean(centered * centered, axis=2, keepdims=True)
    inv = lax.rsqrt(var_val + eps)
    normed = centered * inv
    flat_norm = (normed * gain + shift).astype(jnp.bfloat16).reshape(cells, chans)
    flat_cot = cotangent.reshape(cells, chans)
    hidden = jnp.dot(flat_norm, up_full, preferred_element_type=jnp.float32) + bias_up
    act, slope = gelu_parts(hidden)
    act = act.astype(jnp.bfloat16)
    mixed = jnp.dot(act, down_full, preferred_element_type=jnp.float32)
    block_out = (features.astype(jnp.float32) + (mixed + bias_down).reshape(height, width, chans)).astype(jnp.bfloat16)
    kind = jnp.bfloat16
    down_part = (
        lax.dot_general(act, flat_cot, (((0,), (0,)), ((), ())), preferred_element_type=jnp.float32) * scale
    ).astype(kind)
    dact = lax.dot_general(flat_cot, down_full, (((1,), (1,)), ((), ())), preferred_element_type=jnp.float32)
    dhidden = (dact * slope).astype(jnp.bfloat16)
    up_part = (
        lax.dot_general(flat_norm, dhidden, (((0,), (0,)), ((), ())), preferred_element_type=jnp.float32) * scale
    ).astype(kind)
    dnorm = lax.dot_general(dhidden, up_full, (((1,), (1,)), ((), ())), preferred_element_type=jnp.float32)
    dnorm = dnorm.reshape(height, width, chans)
    down_bias_term = jnp.sum(flat_cot.astype(jnp.float32), axis=0)
    up_bias_term = jnp.sum(dhidden.astype(jnp.float32), axis=0)
    gain_term = jnp.sum(dnorm * normed, axis=(0, 1))
    shift_term = jnp.sum(dnorm, axis=(0, 1))
    scaled = dnorm * gain
    dconv = inv * (
        scaled
        - jnp.mean(scaled, axis=2, keepdims=True)
        - normed * jnp.mean(scaled * normed, axis=2, keepdims=True)
    )
    dconv = dconv.astype(jnp.bfloat16)
    forward = [(i, i + 1) for i in range(devices - 1)]
    backward = [(i + 1, i) for i in range(devices - 1)]
    low = lax.ppermute(dconv[height - HALO :], "row", forward)
    high = lax.ppermute(dconv[:HALO], "row", backward)
    dconv_wide = dconv.astype(jnp.float32)
    tap_terms = []
    for first in range(7):
        for second in range(7):
            tap_terms.append(
                jnp.sum(dconv_wide * padded[first : first + height, second : second + width, :], axis=(0, 1))
            )
    conv_bias_term = jnp.sum(dconv_wide, axis=(0, 1))
    terms = jnp.concatenate(
        [
            jnp.stack(tap_terms + [conv_bias_term, gain_term, shift_term, down_bias_term], axis=0),
            up_bias_term.reshape(devices, ratio, own).transpose(1, 0, 2).reshape(ratio, chans),
        ],
        axis=0,
    ) * scale
    terms = jnp.pad(terms, ((0, filled - rows), (0, 0)))
    terms = terms.reshape(filled, devices, own).transpose(1, 0, 2).reshape(devices, filled * own // LANES, LANES)
    grad_up, grad_down, own_terms = scatter(
        ring,
        up_part.reshape(ring.chips, 2, chans // devices, units),
        down_part.reshape(ring.chips, 2, units // devices, chans),
        terms,
    )
    own_terms = own_terms.reshape(filled, own)
    back_rim = jnp.concatenate([low, dconv, high], axis=0)
    back_pad = jnp.pad(back_rim.astype(jnp.float32), ((0, 0), (3, 3), (0, 0)))
    grad_features = (
        cotangent.astype(jnp.float32) + depth_conv(back_pad, kernel, height, width, True)
    ).astype(jnp.bfloat16)
    return (
        block_out,
        grad_features,
        grad_up,
        grad_down,
        own_terms[:taps],
        own_terms[taps],
        own_terms[taps + 1],
        own_terms[taps + 2],
        own_terms[taps + 4 : taps + 4 + ratio].reshape(ratio * own),
        own_terms[taps + 3],
    )


def solution(mesh):
    ring = Ring(mesh.shape["row"], fold_of(mesh))
    placed = (
        P(("groups", "row"), None, None),
        P(("groups", "row"), None, None),
        P(None, "row"),
        P("row"),
        P("row"),
        P("row"),
        P("row", None),
        P("row"),
        P("row", None),
        P("row"),
    )
    return jax.shard_map(
        functools.partial(per_device, ring),
        mesh=mesh,
        in_specs=placed,
        out_specs=(
            P(("groups", "row"), None, None),
            P(("groups", "row"), None, None),
            P(("groups", "row"), None),
            P(("groups", "row"), None),
            P("groups", "row"),
            P(("groups", "row")),
            P(("groups", "row")),
            P(("groups", "row")),
            P(("groups", "row")),
            P(("groups", "row")),
        ),
        check_vma=False,
    )
```

time: 337 us -> 120 us (0.36)
  blocking collectives: 133 us -> 0 us
  waiting for transfers between devices: 126 us -> 0.01 us
  Pallas kernels: 0 us -> 69.8 us
  between operations: 16.9 us -> 1.62 us
  matrix products: 18.4 us -> 10.8 us
    reduce_scatter x2 -> x0, waiting for transfers between devices: 124 us -> none  [the longest x1 76.1 us: per_device(): lax.psum_scatter(down_full, 'row', scatter_dimension=0, tiled=True)]
    unnamed x2 -> x0, blocking collectives: 89.8 us -> none
    pallas_call x0 -> x2, Pallas kernels: none -> 69.8 us  [the longest x1 37.7 us: gather(): pl.pallas_call(functools.partial(gather_kernel, ring), out_shape=(jax.Sha...]
    all_gather x2 -> x0, blocking collectives: 43.2 us -> none  [the longest x1 25.6 us: per_device(): lax.all_gather(depth_weight, 'row', axis=1, tiled=True)]
    dot_general x5, matrix products: 15.7 us -> 8.74 us  [the longest x1 2.29 us: per_device(): mixed = jnp.dot(act, down_full, preferred_element_type=jnp.float32)]
    slice x3 -> x2, local copies, waits for them, and re-layouts: 6.92 us -> 0.82 us  [depth_conv(): kernel[first * 7 + second]]
    reshape x0 -> x9, local copies, waits for them, and re-layouts: none -> 4.92 us  [the longest x1 1.04 us: per_device(): all_small = all_small.reshape(devices, filled, own).transpose(1, 0, 2)]
    unnamed x155 -> x121, local copies, waits for them, and re-layouts: 7.34 us -> 3.18 us
  transfers between devices with their start and end apart: 9 -> 2, of which waited for: 2 -> 0; matrix products, arithmetic and copies ran while one was open for 11% -> 11% of each run, Pallas kernels for 0% -> 27%
where the time goes in v1:
time: 120 us; the launch traced here: 119 us
  Pallas kernels  69.8 us (58%)
  local copies, waits for them, and re-layouts  18.6 us (16%)
  other arithmetic  14.9 us (12%)
  matrix products  10.8 us (9%)
  starting transfers between devices  3.76 us (3%)
  between operations  1.62 us (1%)
    pallas_call x1, Pallas kernels, gather(): pl.pallas_call(functools.partial(gather_kernel, ring), out_shape=(jax.Sha...  37.7 us
    pallas_call x1, Pallas kernels, scatter(): pl.pallas_call(functools.partial(scatter_kernel, ring), out_shape=(jax.Sh...  32 us
    reduce_sum x1, other arithmetic, per_device(): mean_val = jnp.mean(conv, axis=2, keepdims=True)  4.73 us
    convert_element_type x1, other arithmetic, per_device(): grad_features = (cotangent.astype(jnp.float32) + depth_conv(back_pad, ker...  4.67 us
    reduce_sum x3, other arithmetic, per_device(): jnp.sum(dconv_wide * padded[first:first + height, second:second + width,...  4.06 us
    mul x49, local copies, waits for them, and re-layouts, depth_conv(): padded[top:top + height, left:left + width, :] * kernel[first * 7 + second]  3.81 us
    unnamed x121, local copies, waits for them, and re-layouts  3.18 us
  transfers between devices with their start and end apart: 2, of which 0 were waited for; matrix products, arithmetic and copies ran while one was open for 11% of the time, Pallas kernels for 27%

profile of v1, /device:TPU:0, one launch (start us, length us, event | category | flops | bytes accessed | tf_op | source)
XLA Modules:
  0.0 119.5 jit_solution(11431245640978969061)
XLA Ops:
  0.6 0.7 reshape.258
  1.4 0.1 copy.40
  1.5 0.8 copy.36
  2.2 0.8 copy.37
  3.0 0.8 copy.38
  3.8 0.8 copy.39
  4.5 0.8 concatenate.12
  5.3 0.1 copy.46
  5.5 0.7 reshape.259.small
  6.1 37.7 %gather.1 = (bf16[16,32,2048]{2,1,0:T(8,128)(2,1)}, bf16[16,128,512]{2,1,0:T(8,128)(2,1)}, bf16[16,16,128]{2,1,0:T(8,128)(2,1)}, bf16[2,3,64,512]{3,2,1,0:T(8,128)(2,1)}) custom-call(bf16[32,2048]{1,0:T(8,128)(2,1)} %up.1, bf16[128,512]{1,0:T(8,128)(2,1)} %down.1, bf16[16,128]{1,0:T(8,128)(2,1)} %reshape.259.small, bf16[4,64,512]{2,1,0:T(8,128)(2,1)} %feat.1), custom_call_target="tpu_custom_call" | custom-call | tf_op jit(solution)/shard_map/gather/pallas_call | solution.py:304
  43.9 1.0 reshape.260
  45.0 0.4 slice_reduce_fusion.51
  45.4 0.4 slice_reduce_fusion
  45.8 0.4 slice_reduce_fusion.52
  46.3 0.1 reshape.274
  46.4 0.1 mul.1035
  49.2 0.1 mul.1125
  49.3 0.1 mul.1122
  49.4 0.1 mul.1119
  49.5 0.1 mul.1116
  49.5 0.1 mul.1113
  49.6 0.1 mul.1110
  49.7 0.1 mul.1107
  49.8 0.1 mul.1104
  49.9 0.1 mul.1101
  49.9 0.1 mul.1098
  50.0 0.1 mul.1095
  50.1 0.1 mul.1092
  50.2 0.1 mul.1089
  50.3 0.1 mul.1086
  50.3 0.1 add.413
  50.5 0.1 maximum_convert_fusion
  50.6 4.7 %fusion.146 = (f32[4,64]{1,0:T(4,128)S(1)}, f32[4,64,512]{2,1,0:T(8,128)S(1)}) fusion(f32[512]{0:T(512)S(1)} %add.408, f32[512]{0:T(512)S(1)} %mul.1176, f32[512]{0:T(512)S(1)} %mul.1173, f32[512]{0:T(512)S(1)} %mul.1170, f32[512]{0:T(512)S(1)} %mul.1167, f32[10,64,512]{2,1,0:T(8,128)S(1)} %maximum_convert_fusion, f32[512]{0:T(512)S(1)} %mul.1164, ...), kind=kLoop, calls=%fused_computation.375 | loop fusion | flops 12975872 | bytes 5608448 | tf_op jit(solution)/shard_map/reduce_sum | solution.py:414
  55.5 0.2 multiply_reduce_fusion.2
  55.7 0.2 add_convert_fusion.1
  55.9 1.0 multiply_convert_fusion.2
  57.0 0.6 copy-done.57
  57.6 2.0 %convert_reduce_fusion.1 = (f32[2048]{0:T(1024)}, bf16[256,2048]{1,0:T(8,128)(2,1)S(1)}) fusion(f32[256,2048]{1,0:T(8,128)S(1)} %get-tuple-element.163, bf16[2048,512]{1,0:T(8,128)(2,1)S(1)} %bitcast.175, bf16[256,512]{1,0:T(8,128)(2,1)S(1)} %bitcast.111), kind=kOutput, calls=%fused_computation.61 | convolution fusion | flops 543160320 | bytes 5513216 | tf_op jit(solution)/shard_map/dot_general | solution.py:430
  59.5 1.4 %multiply_reduce_fusion = (f32[512]{0:T(512)}, f32[4,64]{1,0:T(4,128)S(1)}, f32[4,64]{1,0:T(4,128)S(1)}, f32[512]{0:T(512)}, f32[4,64,512]{2,1,0:T(8,128)S(1)}) fusion(f32[4,64,512]{2,1,0:T(8,128)S(1)} %get-tuple-element.153, f32[4,64]{1,0:T(4,128)S(1)} %add_rsqrt_fusion, f32[4,64]{1,0:T(4,128)S(1)} %broadcast_multiply_fusion.3, f32[512]{0:T(512)S(1)} %mul.1182, ...), kind=kOutput, calls=%fused_computation.300 | convolution fusion | flops 538049024 | bytes 4204544 | tf_op jit(solution)/shard_map/dot_general | solution.py:435
  61.0 2.2 %fusion.144 = (f32[512]{0:T(512)}, f32[512]{0:T(512)}, f32[512]{0:T(512)}, f32[512]{0:T(512)}, f32[512]{0:T(512)}, /*index=5*/f32[512]{0:T(512)}, f32[512]{0:T(5...) fusion(f32[10,64,512]{2,1,0:T(8,128)S(1)} %maximum_convert_fusi, ...), kind=kLoop, calls=%fused_computation.291 | loop fusion | flops 5889024 | bytes 3717120 | tf_op jit(solution)/shard_map/reduce_sum | solution.py:457
  63.2 2.3 %collective-permute-start = (bf16[3,64,512]{2,1,0:T(8,128)(2,1)S(1)}, bf16[3,64,512]{2,1,0:T(8,128)(2,1)S(1)}, u32[]{:S(2)}, u32[]{:S(2)}) collective-permute-start(bf16[3,64,512]{2,1,0:T(8,128)(2,1)S(1)} %get-tuple-element.156), channel_id=1, source_target_pairs={{0,1},{1,2},{2,3},{3,4},{4,5},{5,6},{6,7},{7,8},{8,9},{9,10},{10,1... | collective-permute-start | bytes 589832 | tf_op jit(solution)/shard_map/ppermute | solution.py:450
  65.5 1.5 %collective-permute-start.1 = (bf16[3,64,512]{2,1,0:T(8,128)(2,1)S(1)}, bf16[3,64,512]{2,1,0:T(8,128)(2,1)S(1)}, u32[]{:S(2)}, u32[]{:S(2)}) collective-permute-start(bf16[3,64,512]{2,1,0:T(8,128)(2,1)S(1)} %get-tuple-element.157), channel_id=1, source_target_pairs={{1,0},{2,1},{3,2},{4,3},{5,4},{6,5},{7,6},{8,7},{9,8},{10,9},{11,1... | collective-permute-start | bytes 589832 | tf_op jit(solution)/shard_map/ppermute | solution.py:451
  67.0 0.8 fusion.143
  67.8 1.0 fusion.145
  69.1 2.0 %multiply_convert_fusion.1 = bf16[512,2048]{1,0:T(8,128)(2,1)} fusion(bf16[256,512]{1,0:T(8,128)(2,1)S(1)} %bitcast.114, bf16[256,2048]{1,0:T(8,128)(2,1)S(1)} %get-tuple-element.166), kind=kOutput, calls=%fused_computation.51 | convolution fusion | flops 538968064 | bytes 3407872 | tf_op jit(solution)/shard_map/dot_general | solution.py:433
  71.1 0.1 reshape.268
  71.2 0.1 reshape.269
  71.5 0.4 concatenate.15
  71.9 0.1 copy.47
  72.1 0.2 copy.44
  72.3 0.8 reshape.271.small
  73.1 2.1 %multiply_convert_fusion = bf16[2048,512]{1,0:T(8,128)(2,1)} fusion(bf16[256,2048]{1,0:T(8,128)(2,1)S(1)} %get-tuple-element.162, bf16[256,512]{1,0:T(8,128)(2,1)S(1)} %bitcast.112), kind=kOutput, calls=%fused_computation.50 | convolution fusion | flops 538968064 | bytes 3407872 | tf_op jit(solution)/shard_map/dot_general | solution.py:428
  75.2 32.0 %scatter.1 = (f32[32,2048]{1,0:T(8,128)}, f32[128,512]{1,0:T(8,128)}, f32[16,128]{1,0:T(8,128)}) custom-call(bf16[8,2,32,2048]{3,2,1,0:T(8,128)(2,1)} %bitcast.107, bf16[8,2,128,512]{3,2,1,0:T(8,128)(2,1)} %bitcast.108, f32[16,16,128]{2,1,0:T(8,128)} %reshape.271.small), custom_call_target="tpu_custom_call" | custom-call | tf_op jit(solution)/shard_map/scatter/pallas_call | solution.py:332
  107.2 0.8 reshape.272
  108.0 0.1 add.420
  108.1 2.3 %convolution_add_fusion.1 = f32[256,512]{1,0:T(8,128)S(1)} fusion(bf16[256,2048]{1,0:T(8,128)(2,1)S(1)} %get-tuple-element.162, bf16[2048,512]{1,0:T(8,128)(2,1)} %bitcast.174, f32[512]{0:T(512)S(1)} %add.420), kind=kOutput, calls=%fused_computation.148 | convolution fusion | flops 537001984 | bytes 3672064 | tf_op jit(solution)/shard_map/dot_general | solution.py:424
  110.5 0.8 add_convert_fusion
  111.3 0.6 reshape.273
  111.9 0.7 copy.45
  112.6 0.5 slice_bitcast_fusion.2
  113.1 0.1 maximum_convert_fusion.1
  113.4 4.7 %fusion.6 = bf16[4,64,512]{2,1,0:T(8,128)(2,1)} fusion(bf16[4,64,512]{2,1,0:T(8,128)(2,1)S(1)} %copy-done.2, f32[10,64,512]{2,1,0:T(8,128)S(1)} %maximum_convert_fusion.1, f32[512]{0:T(512)S(1)} %mul.1176, f32[512]{0:T(512)S(1)} %mul.1173, f32[512]{0:T(512)S(1)} %mul.1170, f32[512]{0:T(512)S(1)} %mul.1167, f32[512]{0:T(512)S(1)} %mul.1164, ...), kind=kLoop, calls=%fused_computation.153 | loop fusion | flops 13107200 | bytes 5605376 | tf_op jit(solution)/shard_map/convert_element_type | solution.py:480
  118.1 0.7 copy.50
  118.8 0.7 copy.51
  (167 shorter events, 3.3 us)
Async XLA Ops:
  2.2 48.3 %copy-start = (bf16[4,64,512]{2,1,0:T(8,128)(2,1)S(1)}, bf16[4,64,512]{2,1,0:T(8,128)(2,1)}, u32[]{:S(2)}) copy-start(bf16[4,64,512]{2,1,0:T(8,128)(2,1)} %feat.1) | copy-start | bytes 786436
  43.9 2.4 %copy-start.3 = (bf16[2,3,64,512]{3,2,1,0:T(8,128)(2,1)S(1)}, bf16[2,3,64,512]{3,2,1,0:T(8,128)(2,1)}, u32[]{:S(2)}) copy-start(bf16[2,3,64,512]{3,2,1,0:T(8,128)(2,1)} %get-tuple-element.17) | copy-start | bytes 1179652
  49.2 6.2 %copy-start.6 = (f32[512]{0:T(512)}, f32[512]{0:T(512)S(1)}, u32[]{:S(2)}) copy-start(f32[512]{0:T(512)S(1)} %mul.1128) | copy-start | bytes 6148
  49.3 6.1 %copy-start.8 = (f32[512]{0:T(512)}, f32[512]{0:T(512)S(1)}, u32[]{:S(2)}) copy-start(f32[512]{0:T(512)S(1)} %mul.1125) | copy-start | bytes 6148
  49.4 6.0 %copy-start.10 = (f32[512]{0:T(512)}, f32[512]{0:T(512)S(1)}, u32[]{:S(2)}) copy-start(f32[512]{0:T(512)S(1)} %mul.1122) | copy-start | bytes 6148
  49.5 5.9 %copy-start.12 = (f32[512]{0:T(512)}, f32[512]{0:T(512)S(1)}, u32[]{:S(2)}) copy-start(f32[512]{0:T(512)S(1)} %mul.1119) | copy-start | bytes 6148
  49.5 5.8 %copy-start.14 = (f32[512]{0:T(512)}, f32[512]{0:T(512)S(1)}, u32[]{:S(2)}) copy-start(f32[512]{0:T(512)S(1)} %mul.1116) | copy-start | bytes 6148
  49.6 5.8 %copy-start.16 = (f32[512]{0:T(512)}, f32[512]{0:T(512)S(1)}, u32[]{:S(2)}) copy-start(f32[512]{0:T(512)S(1)} %mul.1113) | copy-start | bytes 6148
  49.7 5.7 %copy-start.18 = (f32[512]{0:T(512)}, f32[512]{0:T(512)S(1)}, u32[]{:S(2)}) copy-start(f32[512]{0:T(512)S(1)} %mul.1110) | copy-start | bytes 6148
  49.8 5.6 %copy-start.20 = (f32[512]{0:T(512)}, f32[512]{0:T(512)S(1)}, u32[]{:S(2)}) copy-start(f32[512]{0:T(512)S(1)} %mul.1107) | copy-start | bytes 6148
  49.9 5.6 %copy-start.22 = (f32[512]{0:T(512)}, f32[512]{0:T(512)S(1)}, u32[]{:S(2)}) copy-start(f32[512]{0:T(512)S(1)} %mul.1104) | copy-start | bytes 6148
  49.9 5.5 %copy-start.24 = (f32[512]{0:T(512)}, f32[512]{0:T(512)S(1)}, u32[]{:S(2)}) copy-start(f32[512]{0:T(512)S(1)} %mul.1101) | copy-start | bytes 6148
  50.0 5.4 %copy-start.26 = (f32[512]{0:T(512)}, f32[512]{0:T(512)S(1)}, u32[]{:S(2)}) copy-start(f32[512]{0:T(512)S(1)} %mul.1098) | copy-start | bytes 6148
  50.1 5.4 %copy-start.28 = (f32[512]{0:T(512)}, f32[512]{0:T(512)S(1)}, u32[]{:S(2)}) copy-start(f32[512]{0:T(512)S(1)} %mul.1095) | copy-start | bytes 6148
  50.2 5.3 %copy-start.30 = (f32[512]{0:T(512)}, f32[512]{0:T(512)S(1)}, u32[]{:S(2)}) copy-start(f32[512]{0:T(512)S(1)} %mul.1092) | copy-start | bytes 6148
  50.3 5.2 %copy-start.32 = (f32[512]{0:T(512)}, f32[512]{0:T(512)S(1)}, u32[]{:S(2)}) copy-start(f32[512]{0:T(512)S(1)} %mul.1089) | copy-start | bytes 6148
  50.3 5.1 %copy-start.34 = (f32[512]{0:T(512)}, f32[512]{0:T(512)S(1)}, u32[]{:S(2)}) copy-start(f32[512]{0:T(512)S(1)} %mul.1086) | copy-start | bytes 6148
  50.6 5.3 %copy-start.1 = (bf16[16,32,2048]{2,1,0:T(8,128)(2,1)S(1)}, bf16[16,32,2048]{2,1,0:T(8,128)(2,1)}, u32[]{:S(2)}) copy-start(bf16[16,32,2048]{2,1,0:T(8,128)(2,1)} %get-tuple-element.19) | copy-start | bytes 6291460
  55.9 1.1 copy-start.2
  55.9 1.7 %copy-start.57 = (bf16[16,128,512]{2,1,0:T(8,128)(2,1)S(1)}, bf16[16,128,512]{2,1,0:T(8,128)(2,1)}, u32[]{:S(2)}) copy-start(bf16[16,128,512]{2,1,0:T(8,128)(2,1)} %get-tuple-element.20) | copy-start | bytes 6291460
  63.2 49.9 %collective-permute-start = (bf16[3,64,512]{2,1,0:T(8,128)(2,1)S(1)}, bf16[3,64,512]{2,1,0:T(8,128)(2,1)S(1)}, u32[]{:S(2)}, u32[]{:S(2)}) collective-permute-start(bf16[3,64,512]{2,1,0:T(8,128)(2,1)S(1)} %get-tuple-element.156), channel_id=1, source_target_pairs={{0,1},{1,2},{2,3},{3,4},{4,5},{5,6},{6,7},{7,8},{8,9},{9,10},{10,1... | collective-permute-start | bytes 589832 | tf_op jit(solution)/shard_map/ppermute | solution.py:450
  65.5 47.6 %collective-permute-start.1 = (bf16[3,64,512]{2,1,0:T(8,128)(2,1)S(1)}, bf16[3,64,512]{2,1,0:T(8,128)(2,1)S(1)}, u32[]{:S(2)}, u32[]{:S(2)}) collective-permute-start(bf16[3,64,512]{2,1,0:T(8,128)(2,1)S(1)} %get-tuple-element.157), channel_id=1, source_target_pairs={{1,0},{2,1},{3,2},{4,3},{5,4},{6,5},{7,6},{8,7},{9,8},{10,9},{11,1... | collective-permute-start | bytes 589832 | tf_op jit(solution)/shard_map/ppermute | solution.py:451
  68.9 2.3 %copy-start.54 = (f32[2048]{0:T(1024)S(1)}, f32[2048]{0:T(1024)}, u32[]{:S(2)}) copy-start(f32[2048]{0:T(1024)} %get-tuple-element.165) | copy-start | bytes 24580
  68.9 2.4 %copy-start.36 = (f32[512]{0:T(512)S(1)}, f32[512]{0:T(512)}, u32[]{:S(2)}) copy-start(f32[512]{0:T(512)} %get-tuple-element.62) | copy-start | bytes 6148
  68.9 2.4 %copy-start.37 = (f32[512]{0:T(512)S(1)}, f32[512]{0:T(512)}, u32[]{:S(2)}) copy-start(f32[512]{0:T(512)} %get-tuple-element.63) | copy-start | bytes 6148
  68.9 2.4 %copy-start.38 = (f32[512]{0:T(512)S(1)}, f32[512]{0:T(512)}, u32[]{:S(2)}) copy-start(f32[512]{0:T(512)} %get-tuple-element.64) | copy-start | bytes 6148
  68.9 2.4 %copy-start.39 = (f32[512]{0:T(512)S(1)}, f32[512]{0:T(512)}, u32[]{:S(2)}) copy-start(f32[512]{0:T(512)} %get-tuple-element.65) | copy-start | bytes 6148
  68.9 2.4 %copy-start.40 = (f32[512]{0:T(512)S(1)}, f32[512]{0:T(512)}, u32[]{:S(2)}) copy-start(f32[512]{0:T(512)} %get-tuple-element.66) | copy-start | bytes 6148
  69.0 2.4 %copy-start.41 = (f32[512]{0:T(512)S(1)}, f32[512]{0:T(512)}, u32[]{:S(2)}) copy-start(f32[512]{0:T(512)} %get-tuple-element.67) | copy-start | bytes 6148
  69.0 2.4 %copy-start.42 = (f32[512]{0:T(512)S(1)}, f32[512]{0:T(512)}, u32[]{:S(2)}) copy-start(f32[512]{0:T(512)} %get-tuple-element.68) | copy-start | bytes 6148
  69.0 2.4 %copy-start.43 = (f32[512]{0:T(512)S(1)}, f32[512]{0:T(512)}, u32[]{:S(2)}) copy-start(f32[512]{0:T(512)} %get-tuple-element.69) | copy-start | bytes 6148
  69.0 2.4 %copy-start.44 = (f32[512]{0:T(512)S(1)}, f32[512]{0:T(512)}, u32[]{:S(2)}) copy-start(f32[512]{0:T(512)} %get-tuple-element.70) | copy-start | bytes 6148
  69.0 2.4 %copy-start.45 = (f32[512]{0:T(512)S(1)}, f32[512]{0:T(512)}, u32[]{:S(2)}) copy-start(f32[512]{0:T(512)} %get-tuple-element.71) | copy-start | bytes 6148
  69.0 2.4 %copy-start.46 = (f32[512]{0:T(512)S(1)}, f32[512]{0:T(512)}, u32[]{:S(2)}) copy-start(f32[512]{0:T(512)} %get-tuple-element.72) | copy-start | bytes 6148
  69.0 2.4 %copy-start.47 = (f32[512]{0:T(512)S(1)}, f32[512]{0:T(512)}, u32[]{:S(2)}) copy-start(f32[512]{0:T(512)} %get-tuple-element.73) | copy-start | bytes 6148
  69.0 2.4 %copy-start.48 = (f32[512]{0:T(512)S(1)}, f32[512]{0:T(512)}, u32[]{:S(2)}) copy-start(f32[512]{0:T(512)} %get-tuple-element.74) | copy-start | bytes 6148
  69.0 2.4 %copy-start.49 = (f32[512]{0:T(512)S(1)}, f32[512]{0:T(512)}, u32[]{:S(2)}) copy-start(f32[512]{0:T(512)} %get-tuple-element.75) | copy-start | bytes 6148
  69.0 2.4 %copy-start.50 = (f32[512]{0:T(512)S(1)}, f32[512]{0:T(512)}, u32[]{:S(2)}) copy-start(f32[512]{0:T(512)} %get-tuple-element.76) | copy-start | bytes 6148
  69.1 2.4 %copy-start.51 = (f32[512]{0:T(512)S(1)}, f32[512]{0:T(512)}, u32[]{:S(2)}) copy-start(f32[512]{0:T(512)} %get-tuple-element.77) | copy-start | bytes 6148
  69.1 2.4 %copy-start.52 = (f32[512]{0:T(512)S(1)}, f32[512]{0:T(512)}, u32[]{:S(2)}) copy-start(f32[512]{0:T(512)} %get-tuple-element.78) | copy-start | bytes 6148
  69.1 2.4 %copy-start.53 = (f32[512]{0:T(512)S(1)}, f32[512]{0:T(512)}, u32[]{:S(2)}) copy-start(f32[512]{0:T(512)} %get-tuple-element.79) | copy-start | bytes 6148
  69.1 2.4 %copy-start.55 = (f32[512]{0:T(512)S(1)}, f32[512]{0:T(512)}, u32[]{:S(2)}) copy-start(f32[512]{0:T(512)} %get-tuple-element.93) | copy-start | bytes 6148
  69.1 2.4 %copy-start.56 = (f32[512]{0:T(512)S(1)}, f32[512]{0:T(512)}, u32[]{:S(2)}) copy-start(f32[512]{0:T(512)} %get-tuple-element.96) | copy-start | bytes 6148
  110.4 2.8 %copy-start.7 = (f32[512]{0:T(512)S(1)}, f32[512]{0:T(512)}, u32[]{:S(2)}) copy-start(f32[512]{0:T(512)} %copy-done.6) | copy-start | bytes 6148
  110.4 2.8 %copy-start.9 = (f32[512]{0:T(512)S(1)}, f32[512]{0:T(512)}, u32[]{:S(2)}) copy-start(f32[512]{0:T(512)} %copy-done.8) | copy-start | bytes 6148
  110.4 2.8 %copy-start.11 = (f32[512]{0:T(512)S(1)}, f32[512]{0:T(512)}, u32[]{:S(2)}) copy-start(f32[512]{0:T(512)} %copy-done.10) | copy-start | bytes 6148
  110.4 2.8 %copy-start.13 = (f32[512]{0:T(512)S(1)}, f32[512]{0:T(512)}, u32[]{:S(2)}) copy-start(f32[512]{0:T(512)} %copy-done.12) | copy-start | bytes 6148
  110.4 2.8 %copy-start.15 = (f32[512]{0:T(512)S(1)}, f32[512]{0:T(512)}, u32[]{:S(2)}) copy-start(f32[512]{0:T(512)} %copy-done.14) | copy-start | bytes 6148
  110.4 2.8 %copy-start.17 = (f32[512]{0:T(512)S(1)}, f32[512]{0:T(512)}, u32[]{:S(2)}) copy-start(f32[512]{0:T(512)} %copy-done.16) | copy-start | bytes 6148
  110.5 2.8 %copy-start.19 = (f32[512]{0:T(512)S(1)}, f32[512]{0:T(512)}, u32[]{:S(2)}) copy-start(f32[512]{0:T(512)} %copy-done.18) | copy-start | bytes 6148
  110.5 2.8 %copy-start.21 = (f32[512]{0:T(512)S(1)}, f32[512]{0:T(512)}, u32[]{:S(2)}) copy-start(f32[512]{0:T(512)} %copy-done.20) | copy-start | bytes 6148
  110.5 2.8 %copy-start.23 = (f32[512]{0:T(512)S(1)}, f32[512]{0:T(512)}, u32[]{:S(2)}) copy-start(f32[512]{0:T(512)} %copy-done.22) | copy-start | bytes 6148
  110.5 2.8 %copy-start.25 = (f32[512]{0:T(512)S(1)}, f32[512]{0:T(512)}, u32[]{:S(2)}) copy-start(f32[512]{0:T(512)} %copy-done.24) | copy-start | bytes 6148
  110.5 2.8 %copy-start.27 = (f32[512]{0:T(512)S(1)}, f32[512]{0:T(512)}, u32[]{:S(2)}) copy-start(f32[512]{0:T(512)} %copy-done.26) | copy-start | bytes 6148
  110.5 2.8 %copy-start.29 = (f32[512]{0:T(512)S(1)}, f32[512]{0:T(512)}, u32[]{:S(2)}) copy-start(f32[512]{0:T(512)} %copy-done.28) | copy-start | bytes 6148
  110.5 2.8 %copy-start.31 = (f32[512]{0:T(512)S(1)}, f32[512]{0:T(512)}, u32[]{:S(2)}) copy-start(f32[512]{0:T(512)} %copy-done.30) | copy-start | bytes 6148
  110.5 2.8 %copy-start.33 = (f32[512]{0:T(512)S(1)}, f32[512]{0:T(512)}, u32[]{:S(2)}) copy-start(f32[512]{0:T(512)} %copy-done.32) | copy-start | bytes 6148
  110.5 2.8 %copy-start.35 = (f32[512]{0:T(512)S(1)}, f32[512]{0:T(512)}, u32[]{:S(2)}) copy-start(f32[512]{0:T(512)} %copy-done.34) | copy-start | bytes 6148
  113.4 4.7 %copy-start.5 = (f32[32,2048]{1,0:T(8,128)S(1)}, f32[32,2048]{1,0:T(8,128)}, u32[]{:S(2)}) copy-start(f32[32,2048]{1,0:T(8,128)} %get-tuple-element.181) | copy-start | bytes 786436
  113.4 5.4 %copy-start.4 = (f32[128,512]{1,0:T(8,128)S(1)}, f32[128,512]{1,0:T(8,128)}, u32[]{:S(2)}) copy-start(f32[128,512]{1,0:T(8,128)} %get-tuple-element.182) | copy-start | bytes 786436

commit v2 on v1

--- a/solution.py
+++ b/solution.py
@@ -68,9 +68,61 @@
     )
 
 
+LEFT = 8
+
+
+def fill_middle(wide_rows, block):
+    height, width, _ = block.shape
+    wide_rows[...] = jnp.zeros_like(wide_rows)
+    for row in range(height):
+        wide_rows[HALO + row, LEFT : LEFT + width, :] = block[row].astype(jnp.float32)
+
+
+def fill_rims(wide_rows, rim, height, width):
+    for row in range(HALO):
+        wide_rows[row, LEFT : LEFT + width, :] = rim[0, row].astype(jnp.float32)
+        wide_rows[HALO + height + row, LEFT : LEFT + width, :] = rim[1, row].astype(jnp.float32)
+
+
+def conv_row(wide_rows, kernel, row, width, flip, store):
+    chans = wide_rows.shape[2]
+
+    @pl.loop(0, chans // LANES)
+    def _(group):
+        lanes = pl.ds(pl.multiple_of(group * LANES, LANES), LANES)
+        total = jnp.zeros((width, LANES), jnp.float32)
+        for first in range(7):
+            for second in range(7):
+                top, left = (6 - first, 6 - second) if flip else (first, second)
+                tap = first * 7 + second
+                begin = LEFT - HALO + left
+                total = total + wide_rows[row + top, begin : begin + width, lanes] * kernel[tap : tap + 1, lanes]
+        store(lanes, total)
+
+
+def unpack(all_small, wide, devices, own):
+    pieces = LANES // own
+    rows = all_small.shape[1]
+    spot = lax.broadcasted_iota(jnp.int32, (rows, LANES), 1) // own
+    for group in range(devices // pieces):
+        sources = [all_small[group * pieces + part].astype(jnp.float32) for part in range(pieces)]
+        for block in range(pieces):
+            total = jnp.zeros((rows, LANES), jnp.float32)
+            for part in range(pieces):
+                shift = ((part - block) * own) % LANES
+                moved = sources[part] if shift == 0 else pltpu.roll(sources[part], shift, 1)
+                total = jnp.where(spot == part, moved, total)
+            wide[block * rows : (block + 1) * rows, group * LANES : (group + 1) * LANES] = total
+
+
+def rows_at(step, most, height):
+    return [row for row in range(height) if min(2, most) + row * (most - 1) // height == step]
+
+
 def gather_kernel(
-    ring, up, down, small, feat,
-    all_up, all_down, all_small, rim,
+    ring, taps, up, down, small, feat,
+    all_up, all_down, wide, rim, normed, normal_out, inv_out,
+    all_small, wide_rows, conv,
     ring_out, ring_in, pair_out, pair_in, small_out, small_in, rim_out, rim_in, own_sem,
 ):
     devices = ring.devices
@@ -80,7 +132,20 @@
     place = ring.place(chip)
     mine, gathered = (up, down), (all_up, all_down)
     greet_all(me, devices)
-    height = feat.shape[0]
+    height, width, chans = feat.shape
+
+    def normalise(row):
+        def store(lanes, total):
+            conv[:, lanes] = total + wide[taps : taps + 1, lanes]
+
+        conv_row(wide_rows, wide, row, width, False, store)
+        value = conv[...]
+        centered = value - jnp.mean(value, axis=1, keepdims=True)
+        inv = lax.rsqrt(jnp.mean(centered * centered, axis=1, keepdims=True) + eps)
+        unit = centered * inv
+        normed[row] = unit
+        inv_out[row] = inv
+        normal_out[row] = (unit * wide[taps + 1 : taps + 2, :] + wide[taps + 2 : taps + 3, :]).astype(normal_out.dtype)
 
     def lower_rim():
         return send(feat.at[pl.ds(height - HALO, HALO)], rim.at[0], rim_out.at[0], rim_in.at[0], lax.rem(me + 1, devices))
@@ -149,6 +214,7 @@
         if step == 1:
             for flow in (0, 1):
                 hand(flow, 0).start()
+            fill_middle(wide_rows, feat)
             owns = [
                 pltpu.make_async_copy(up, all_up.at[me], own_sem.at[0]),
                 pltpu.make_async_copy(down, all_down.at[me], own_sem.at[1]),
@@ -164,6 +230,26 @@
             @pl.when(me == devices - 1)
             def _():
                 rim[1] = jnp.zeros(rim.shape[1:], rim.dtype)
+
+            owns[2].wait()
+
+            @pl.loop(1, devices)
+            def _(other):
+                small_arrival(other).wait_recv()
+
+            unpack(all_small, wide, devices, chans // devices)
+
+            @pl.when(me < devices - 1)
+            def _():
+                upper_rim().wait_recv()
+
+            @pl.when(me > 0)
+            def _():
+                lower_rim().wait_recv()
+
+            fill_rims(wide_rows, rim, height, width)
+        for row in rows_at(step, ring.most, height):
+            normalise(row)
 
     for flow in flows:
         hops = ring.flows[flow][2]
@@ -179,28 +265,25 @@
 
     @pl.loop(1, devices)
     def _(step):
-        small_arrival(step).wait_recv()
         small_copy(step).wait_send()
 
-    for own in owns:
+    for own in owns[:2]:
         own.wait()
 
     @pl.when(me < devices - 1)
     def _():
         lower_rim().wait_send()
-        upper_rim().wait_recv()
 
     @pl.when(me > 0)
     def _():
         upper_rim().wait_send()
-        lower_rim().wait_recv()
 
 
 def scatter_kernel(
-    ring, up, down, small,
-    own_up, own_down, own_small,
-    half_up, half_down, got_up, got_down, out_up, out_down, got_small,
-    ring_out, ring_in, pair_out, pair_in, small_out, small_in,
+    ring, up, down, small, dconv, wide, cot,
+    own_up, own_down, own_small, grad_feat,
+    half_up, half_down, got_up, got_down, out_up, out_down, got_small, rim, wide_rows,
+    ring_out, ring_in, pair_out, pair_in, small_out, small_in, rim_out, rim_in,
 ):
     devices = ring.devices
     me = lax.axis_index("row")
@@ -211,6 +294,20 @@
     got, out, total = (got_up, got_down), (out_up, out_down), (own_up, own_down)
     greet_all(me, devices)
 
+    height, width, _ = dconv.shape
+
+    def lower_rim():
+        return send(dconv.at[pl.ds(height - HALO, HALO)], rim.at[0], rim_out.at[0], rim_in.at[0], lax.rem(me + 1, devices))
+
+    def upper_rim():
+        return send(dconv.at[pl.ds(0, HALO)], rim.at[1], rim_out.at[1], rim_in.at[1], lax.rem(me + devices - 1, devices))
+
+    def spread(row):
+        def store(lanes, total):
+            grad_feat[row, :, lanes] = (cot[row, :, lanes].astype(jnp.float32) + total).astype(grad_feat.dtype)
+
+        conv_row(wide_rows, wide, row, width, True, store)
+
     def pair(which, offset):
         slot = ring.chip_at(place + offset)
         return send(
@@ -226,6 +323,14 @@
     for offset in order:
         for which in (0, 1):
             pair(which, offset).start()
+
+    @pl.when(me < devices - 1)
+    def _():
+        lower_rim().start()
+
+    @pl.when(me > 0)
+    def _():
+        upper_rim().start()
 
     def small_copy(step):
         target = lax.rem(me + step, devices)
@@ -266,6 +371,28 @@
                     value = value + got[which][side, step - 2].astype(jnp.float32)
                 out[which][side, step - 1] = value.astype(out[which].dtype)
                 hop(flow, step).start()
+        if step == 1:
+            fill_middle(wide_rows, dconv)
+
+            @pl.when(me == 0)
+            def _():
+                rim[0] = jnp.zeros(rim.shape[1:], rim.dtype)
+
+            @pl.when(me == devices - 1)
+            def _():
+                rim[1] = jnp.zeros(rim.shape[1:], rim.dtype)
+
+            @pl.when(me < devices - 1)
+            def _():
+                upper_rim().wait_recv()
+
+            @pl.when(me > 0)
+            def _():
+                lower_rim().wait_recv()
+
+            fill_rims(wide_rows, rim, height, width)
+        for row in rows_at(step, ring.most, height):
+            spread(row)
 
     step_sum = small[me]
     for step in range(1, devices):
@@ -293,25 +420,40 @@
     def _(step):
         small_copy(step).wait_send()
 
+    @pl.when(me < devices - 1)
+    def _():
+        lower_rim().wait_send()
+
+    @pl.when(me > 0)
+    def _():
+        upper_rim().wait_send()
+
 
 def vmem():
     return pl.BlockSpec(memory_space=pltpu.VMEM)
 
 
-def gather(ring, up, down, small, feat):
+def gather(ring, taps, filled, up, down, small, feat):
+    height, width, chans = feat.shape
     devices, most, flows = ring.devices, ring.most, len(ring.flows)
     dma = pltpu.SemaphoreType.DMA
     return pl.pallas_call(
-        functools.partial(gather_kernel, ring),
+        functools.partial(gather_kernel, ring, taps),
         out_shape=(
             jax.ShapeDtypeStruct((devices,) + up.shape, up.dtype),
             jax.ShapeDtypeStruct((devices,) + down.shape, down.dtype),
-            jax.ShapeDtypeStruct((devices,) + small.shape, small.dtype),
+            jax.ShapeDtypeStruct((filled, chans), jnp.float32),
             jax.ShapeDtypeStruct((2, HALO) + feat.shape[1:], feat.dtype),
+            jax.ShapeDtypeStruct(feat.shape, jnp.float32),
+            jax.ShapeDtypeStruct(feat.shape, jnp.bfloat16),
+            jax.ShapeDtypeStruct((height, width, 1), jnp.float32),
         ),
         in_specs=[vmem()] * 4,
-        out_specs=(vmem(),) * 4,
+        out_specs=(vmem(),) * 7,
         scratch_shapes=[
+            pltpu.VMEM((devices,) + small.shape, small.dtype),
+            pltpu.VMEM((height + 2 * HALO, width + 2 * LEFT, chans), jnp.float32),
+            pltpu.VMEM((width, chans), jnp.float32),
             dma((flows, most)), dma((flows, most)),
             dma((flows, most + 1)), dma((flows, most + 1)),
             dma((devices,)), dma((devices,)),
@@ -324,7 +466,8 @@
     )(up, down, small, feat)
 
 
-def scatter(ring, up, down, small):
+def scatter(ring, up, down, small, dconv, wide, cot):
+    height, width, chans = dconv.shape
     devices, most, flows, chips = ring.devices, ring.most, len(ring.flows), ring.chips
     dma = pltpu.SemaphoreType.DMA
     block_up, block_down = up.shape[2:], down.shape[2:]
@@ -335,9 +478,10 @@
             jax.ShapeDtypeStruct(block_up, jnp.float32),
             jax.ShapeDtypeStruct(block_down, jnp.float32),
             jax.ShapeDtypeStruct(small.shape[1:], jnp.float32),
+            jax.ShapeDtypeStruct(cot.shape, cot.dtype),
         ),
-        in_specs=[vmem()] * 3,
-        out_specs=(vmem(),) * 3,
+        in_specs=[vmem()] * 6,
+        out_specs=(vmem(),) * 4,
         scratch_shapes=[
             pltpu.VMEM((chips,) + block_up, kind),
             pltpu.VMEM((chips,) + block_down, kind),
@@ -346,30 +490,24 @@
             pltpu.VMEM((2, most) + block_up, kind),
             pltpu.VMEM((2, most) + block_down, kind),
             pltpu.VMEM(small.shape, jnp.float32),
+            pltpu.VMEM((2, HALO, width, chans), dconv.dtype),
+            pltpu.VMEM((height + 2 * HALO, width + 2 * LEFT, chans), jnp.float32),
             dma((flows, most)), dma((flows, most)),
             dma((2, chips)), dma((2, chips)),
             dma((devices,)), dma((devices,)),
+            dma((2,)), dma((2,)),
         ],
         compiler_params=pltpu.CompilerParams(
             collective_id=1, has_side_effects=True, vmem_limit_bytes=56 * 2**20
         ),
         name="scatter",
-    )(up, down, small)
+    )(up, down, small, dconv, wide, cot)
 
 
 def gelu_parts(value):
     cumulative = 0.5 * (1.0 + lax.erf(value * (1.0 / math.sqrt(2.0))))
     density = jnp.exp(-0.5 * value * value) * (1.0 / math.sqrt(2.0 * math.pi))
     return value * cumulative, cumulative + value * density
-
-
-def depth_conv(padded, kernel, height, width, flip):
-    total = jnp.zeros((height, width, kernel.shape[1]), jnp.float32)
-    for first in range(7):
-        for second in range(7):
-            top, left = (6 - first, 6 - second) if flip else (first, second)
-            total = total + padded[top : top + height, left : left + width, :] * kernel[first * 7 + second]
-    return total
 
 
 def per_device(
@@ -398,25 +536,20 @@
     )
     rows = packed.shape[0]
     filled = -(-rows // 64) * 64
-    packed = jnp.pad(packed, ((0, filled - rows), (0, 0))).reshape(filled * own // LANES, LANES)
-    all_up, all_down, all_small, rim = gather(ring, up_weight, down_weight, packed, features)
+    pieces = LANES // own
+    packed = jnp.pad(packed, ((0, filled - rows), (0, 0)))
+    packed = packed.reshape(pieces, filled // pieces, own).transpose(1, 0, 2).reshape(filled // pieces, LANES)
+    taps = depth_weight.shape[0]
+    all_up, all_down, wide, rim, normed, normal_out, inv = gather(
+        ring, taps, filled, up_weight, down_weight, packed, features
+    )
     up_full = all_up.reshape(chans, units)
     down_full = all_down.reshape(units, chans)
-    all_small = all_small.reshape(devices, filled, own).transpose(1, 0, 2)
-    wide = all_small.reshape(filled, chans).astype(jnp.float32)
-    taps = depth_weight.shape[0]
-    kernel, conv_bias, gain, shift, bias_down = wide[:taps], wide[taps], wide[taps + 1], wide[taps + 2], wide[taps + 3]
-    bias_up = all_small[taps + 4 : taps + 4 + ratio].transpose(1, 0, 2).reshape(units).astype(jnp.float32)
-
+    gain, bias_down = wide[taps + 1], wide[taps + 3]
+    bias_up = wide[taps + 4 : taps + 4 + ratio].reshape(ratio, devices, own).transpose(1, 0, 2).reshape(units)
     rimmed = jnp.concatenate([rim[0], features, rim[1]], axis=0)
     padded = jnp.pad(rimmed.astype(jnp.float32), ((0, 0), (3, 3), (0, 0)))
-    conv = depth_conv(padded, kernel, height, width, False) + conv_bias
-    mean_val = jnp.mean(conv, axis=2, keepdims=True)
-    centered = conv - mean_val
-    var_val = jnp.mean(centered * centered, axis=2, keepdims=True)
-    inv = lax.rsqrt(var_val + eps)
-    normed = centered * inv
-    flat_norm = (normed * gain + shift).astype(jnp.bfloat16).reshape(cells, chans)
+    flat_norm = normal_out.reshape(cells, chans)
     flat_cot = cotangent.reshape(cells, chans)
     hidden = jnp.dot(flat_norm, up_full, preferred_element_type=jnp.float32) + bias_up
     act, slope = gelu_parts(hidden)
@@ -445,10 +578,6 @@
         - normed * jnp.mean(scaled * normed, axis=2, keepdims=True)
     )
     dconv = dconv.astype(jnp.bfloat16)
-    forward = [(i, i + 1) for i in range(devices - 1)]
-    backward = [(i + 1, i) for i in range(devices - 1)]
-    low = lax.ppermute(dconv[height - HALO :], "row", forward)
-    high = lax.ppermute(dconv[:HALO], "row", backward)
     dconv_wide = dconv.astype(jnp.float32)
     tap_terms = []
     for first in range(7):
@@ -466,18 +595,16 @@
     ) * scale
     terms = jnp.pad(terms, ((0, filled - rows), (0, 0)))
     terms = terms.reshape(filled, devices, own).transpose(1, 0, 2).reshape(devices, filled * own // LANES, LANES)
-    grad_up, grad_down, own_terms = scatter(
+    grad_up, grad_down, own_terms, grad_features = scatter(
         ring,
         up_part.reshape(ring.chips, 2, chans // devices, units),
         down_part.reshape(ring.chips, 2, units // devices, chans),
         terms,
+        dconv,
+        wide,
+        cotangent,
     )
     own_terms = own_terms.reshape(filled, own)
-    back_rim = jnp.concatenate([low, dconv, high], axis=0)
-    back_pad = jnp.pad(back_rim.astype(jnp.float32), ((0, 0), (3, 3), (0, 0)))
-    grad_features = (
-        cotangent.astype(jnp.float32) + depth_conv(back_pad, kernel, height, width, True)
-    ).astype(jnp.bfloat16)
     return (
         block_out,
         grad_features,

time: 120 us -> 104 us (0.87)
  other arithmetic: 14.9 us -> 6.32 us
  local copies, waits for them, and re-layouts: 18.6 us -> 12.1 us
  starting transfers between devices: 3.76 us -> 0 us
  Pallas kernels: 69.8 us -> 71.9 us
  matrix products: 10.8 us -> 12.3 us
    convert_element_type x5 -> x0, other arithmetic: 4.99 us -> none  [the longest x1 4.67 us: per_device(): grad_features = (cotangent.astype(jnp.float32) + depth_conv(back_pad, ker...]
    reduce_sum x2 -> x0, other arithmetic: 4.92 us -> none  [the longest x1 4.73 us: per_device(): mean_val = jnp.mean(conv, axis=2, keepdims=True)]
    mul x50 -> x0, local copies, waits for them, and re-layouts: 3.89 us -> none  [the longest x49 3.81 us: depth_conv(): padded[top:top + height, left:left + width, :] * kernel[first * 7 + second]]
    ppermute x2 -> x0, starting transfers between devices: 3.76 us -> none  [the longest x1 2.29 us: per_device(): low = lax.ppermute(dconv[height - HALO:], 'row', forward)]
    broadcast_in_dim x4 -> x0, local copies, waits for them, and re-layouts: 3.05 us -> none  [the longest x1 0.79 us: per_device(): norm_gain[None]]
    pallas_call x1, Pallas kernels: 32 us -> 34.7 us  [scatter(): pl.pallas_call(functools.partial(scatter_kernel, ring), out_shape=(jax.Sh...]
    dot_general x1, matrix products: 1.04 us -> 2.68 us  [per_device(): jnp.dot(flat_norm, up_full, preferred_element_type=jnp.float32) + bias_up]
    dot_general x1, matrix products: 2.29 us -> 0.7 us  [per_device(): mixed = jnp.dot(act, down_full, preferred_element_type=jnp.float32)]
  transfers between devices with their start and end apart: 2 -> 0, of which waited for: 0 -> 0; matrix products, arithmetic and copies ran while one was open for 11% -> 0% of each run, Pallas kernels for 27% -> 0%
where the time goes in v2:
time: 104 us
  Pallas kernels  71.9 us (69%)
  matrix products  12.3 us (12%)
  local copies, waits for them, and re-layouts  12.1 us (12%)
  other arithmetic  6.32 us (6%)
    pallas_call x1, Pallas kernels, gather(): pl.pallas_call(functools.partial(gather_kernel, ring, taps), out_shape=(j...  37.2 us
    pallas_call x1, Pallas kernels, scatter(): pl.pallas_call(functools.partial(scatter_kernel, ring), out_shape=(jax.Sh...  34.7 us
    reduce_sum x3, other arithmetic, per_device(): jnp.sum(dconv_wide * padded[first:first + height, second:second + width,...  4.68 us
    unnamed x40, local copies, waits for them, and re-layouts  3.96 us
    dot_general x1, matrix products, per_device(): lax.dot_general(flat_norm, dhidden, (((0,), (0,)), ((), ())), preferred_e...  3.25 us
    dot_general x1, matrix products, per_device(): jnp.dot(flat_norm, up_full, preferred_element_type=jnp.float32) + bias_up  2.68 us
    dot_general x1, matrix products, per_device(): lax.dot_general(dhidden, up_full, (((1,), (1,)), ((), ())), preferred_ele...  2.18 us

profile of v2, /device:TPU:0, one launch (start us, length us, event | category | flops | bytes accessed | tf_op | source)
XLA Modules:
  0.0 103.5 jit_solution(5790620417712607392)
XLA Ops:
  0.6 0.8 copy.33
  1.4 0.7 reshape.83
  2.2 0.8 concatenate.9
  3.0 0.7 reshape.85.small
  3.7 37.2 %gather.1 = (bf16[16,32,2048]{2,1,0:T(8,128)(2,1)}, bf16[16,128,512]{2,1,0:T(8,128)(2,1)}, f32[64,512]{1,0:T(8,128)}, bf16[2,3,64,512]{3,2,1,0:T(8,128)(2,1)}, f...) custom-call(bf16[32,2048]{1,0:T(8,128)(2,1)} %up.1, bf16[128,512]{1,0:T(8,128)(2,1)} %down.1, ...), custom_call_target="tpu_custom_call" | custom-call | tf_op jit(solution)/shard_map/gather/pallas_call | solution.py:440
  40.9 0.8 slice.187
  41.7 0.1 reshape.88
  41.8 0.1 add.38
  41.9 2.7 %multiply_convert_fusion.2 = (bf16[256,2048]{1,0:T(8,128)(2,1)S(1)}, f32[256,2048]{1,0:T(8,128)S(1)}) fusion(f32[2048]{0:T(1024)S(1)} %add.38, bf16[256,512]{1,0:T(8,128)(2,1)} %bitcast.117, bf16[512,2048]{1,0:T(8,128)(2,1)} %bitcast.109), kind=kOutput, calls=%fused_computation.62 | convolution fusion | flops 540016640 | bytes 5513216 | tf_op jit(solution)/shard_map/dot_general | solution.py:554
  44.6 0.0 copy-done.3
  44.6 0.0 copy-done.14
  44.6 0.0 copy-start.2
  44.6 0.0 copy-start.4
  44.6 1.4 %convert_reduce_fusion.1 = (f32[2048]{0:T(1024)S(1)}, bf16[256,2048]{1,0:T(8,128)(2,1)S(1)}) fusion(f32[256,2048]{1,0:T(8,128)S(1)} %get-tuple-element.116, bf16[2048,512]{1,0:T(8,128)(2,1)S(1)} %bitcast.182, bf16[256,512]{1,0:T(8,128)(2,1)S(1)} %bitcast.114), kind=kOutput, calls=%fused_computation.61 | convolution fusion | flops 543160320 | bytes 5513216 | tf_op jit(solution)/shard_map/dot_general | solution.py:563
  46.0 0.0 copy-start.16
  46.0 1.4 %fusion.55 = (f32[1,512]{1,0:T(1,128)S(1)}, f32[1,512]{1,0:T(1,128)}) fusion(f32[64,512]{1,0:T(8,128)} %get-tuple-element.23.wide), kind=kLoop, calls=%fused_computation.173 | loop fusion | bytes 8192 | tf_op jit(solution)/shard_map/slice | solution.py:548
  47.4 0.0 copy-done.2
  47.4 0.0 copy-done.4
  47.4 0.0 copy-start.1
  47.4 2.2 %multiply_reduce_fusion = (f32[512]{0:T(512)}, f32[4,64]{1,0:T(4,128)S(1)}, f32[4,64]{1,0:T(4,128)S(1)}, f32[512]{0:T(512)}, f32[4,64,512]{2,1,0:T(8,128)}) fusion(f32[4,64,512]{2,1,0:T(8,128)S(1)} %copy-done.4, f32[512]{0:T(512)S(1)} %bitcast.173, bf16[4,64,2048]{2,1,0:T(8,128)(2,1)S(1)} %bitcast.184, bf16[512,2048,1]{1,0,2:T(8,128)(2,1)S(1)} %bitcast.110), kind=kOutput, calls=%fused_computation.158 | convolution fusion | flops 537786880 | bytes 4202496 | tf_op jit(solution)/shard_map/dot_general | solution.py:568
  49.6 0.0 copy-done.16
  49.6 0.6 broadcast_multiply_fusion.1
  50.2 0.0 copy-done.5
  50.2 0.0 copy-done.1
  50.3 0.1 maximum_convert_fusion
  50.4 0.2 copy-done.10
  50.5 0.1 reduce.1
  50.6 2.6 %fusion.53 = (f32[512]{0:T(512)S(1)}, f32[512]{0:T(512)S(1)}, f32[512]{0:T(512)S(1)}, f32[512]{0:T(512)S(1)}, f32[512]{0:T(512)S(1)}, /*index=5*/f32[512]{0:T(51...) fusion(f32[10,64,512]{2,1,0:T(8,128)S(1)} %maximum_convert_fusi, ...), kind=kLoop, calls=%fused_computation.155 | loop fusion | flops 5626880 | bytes 2663424 | tf_op jit(solution)/shard_map/reduce_sum | solution.py:586
  53.2 0.0 copy-start
  53.2 1.4 %fusion.54 = (f32[512]{0:T(512)S(1)}, f32[512]{0:T(512)S(1)}, f32[512]{0:T(512)S(1)}, f32[512]{0:T(512)S(1)}, f32[512]{0:T(512)S(1)}, /*index=5*/f32[512]{0:T(51...) fusion(f32[10,64,512]{2,1,0:T(8,128)S(1)} %maximum_convert_fusi, ...), kind=kLoop, calls=%fused_computation.156 | loop fusion | flops 4840448 | bytes 1609728 | tf_op jit(solution)/shard_map/reduce_sum | solution.py:586
  54.6 0.0 copy-start.11
  54.6 0.0 copy-start.12
  54.6 0.7 fusion.52
  55.4 0.0 copy-done
  55.4 0.0 copy-start.9
  55.4 0.1 reshape.94
  55.5 0.1 reshape.95
  55.6 0.1 convert_reduce_fusion.2
  55.6 0.0 copy-done.11
  55.6 0.0 copy-done.12
  55.6 0.4 concatenate.11
  56.0 0.1 copy.40
  56.2 0.2 copy.38
  56.4 0.8 reshape.97.small
  57.2 0.0 copy-done.9
  57.2 3.3 %multiply_convert_fusion.1 = bf16[512,2048]{1,0:T(8,128)(2,1)} fusion(bf16[256,512]{1,0:T(8,128)(2,1)S(1)} %bitcast.118, bf16[256,2048]{1,0:T(8,128)(2,1)} %copy-done.16), kind=kOutput, calls=%fused_computation.51 | convolution fusion | flops 538968064 | bytes 3407872 | tf_op jit(solution)/shard_map/dot_general | solution.py:566
  60.5 2.1 %multiply_convert_fusion = bf16[2048,512]{1,0:T(8,128)(2,1)} fusion(bf16[256,2048]{1,0:T(8,128)(2,1)S(1)} %get-tuple-element.115, bf16[256,512]{1,0:T(8,128)(2,1)S(1)} %bitcast.115), kind=kOutput, calls=%fused_computation.50 | convolution fusion | flops 538968064 | bytes 3407872 | tf_op jit(solution)/shard_map/dot_general | solution.py:561
  62.6 34.7 %scatter.1 = (f32[32,2048]{1,0:T(8,128)}, f32[128,512]{1,0:T(8,128)}, f32[16,128]{1,0:T(8,128)}, bf16[4,64,512]{2,1,0:T(8,128)(2,1)}) custom-call(bf16[8,2,32,2048]{3,2,1,0:T(8,128)(2,1)} %bitcast.111, bf16[8,2,128,512]{3,2,1,0:T(8,128)(2,1)} %bitcast.112, f32[16,16,128]{2,1,0:T(8,128)} %reshape.97.small, bf16[4,64,512]{2,1,0:T(8,128)(2,1)} %copy-done, ...), custom_call_target="tpu_custom_call" | custom-call | tf_op jit(solution)/shard_map/scatter/pallas_call | solution.py:475
  97.3 0.8 reshape.98
  98.1 0.7 copy.39
  98.8 0.6 reshape.99
  99.4 0.5 slice_bitcast_fusion.2
  99.9 0.0 copy-done.13
  99.9 0.0 copy-done.15
  99.9 0.0 copy-start.7
  99.9 0.0 copy-start.6
  99.9 0.7 convolution_add_fusion.1
  100.6 0.8 add_convert_fusion
  101.4 0.0 copy-done.8
  101.4 0.7 copy.46
  102.1 0.0 copy-done.7
  102.1 0.7 copy.47
  102.8 0.0 copy-done.6
  102.8 0.7 copy.48
  (16 shorter events, 0.1 us)
Async XLA Ops:
  41.9 2.7 %copy-start.3 = (bf16[4,64,512]{2,1,0:T(8,128)(2,1)S(1)}, bf16[4,64,512]{2,1,0:T(8,128)(2,1)}, u32[]{:S(2)}) copy-start(bf16[4,64,512]{2,1,0:T(8,128)(2,1)} %cot.1) | copy-start | bytes 786436
  41.9 2.7 %copy-start.14 = (bf16[16,128,512]{2,1,0:T(8,128)(2,1)S(1)}, bf16[16,128,512]{2,1,0:T(8,128)(2,1)}, u32[]{:S(2)}) copy-start(bf16[16,128,512]{2,1,0:T(8,128)(2,1)} %get-tuple-element.24) | copy-start | bytes 6291460
  44.6 2.8 %copy-start.2 = (bf16[16,32,2048]{2,1,0:T(8,128)(2,1)S(1)}, bf16[16,32,2048]{2,1,0:T(8,128)(2,1)}, u32[]{:S(2)}) copy-start(bf16[16,32,2048]{2,1,0:T(8,128)(2,1)} %get-tuple-element.22) | copy-start | bytes 6291460
  44.6 2.8 %copy-start.4 = (f32[4,64,512]{2,1,0:T(8,128)S(1)}, f32[4,64,512]{2,1,0:T(8,128)}, u32[]{:S(2)}) copy-start(f32[4,64,512]{2,1,0:T(8,128)} %get-tuple-element.26) | copy-start | bytes 1572868
  46.0 3.6 %copy-start.16 = (bf16[256,2048]{1,0:T(8,128)(2,1)}, bf16[256,2048]{1,0:T(8,128)(2,1)S(1)}, u32[]{:S(2)}) copy-start(bf16[256,2048]{1,0:T(8,128)(2,1)S(1)} %get-tuple-element.119) | copy-start | bytes 3145732
  47.4 2.8 %copy-start.5 = (bf16[2,3,64,512]{3,2,1,0:T(8,128)(2,1)S(1)}, bf16[2,3,64,512]{3,2,1,0:T(8,128)(2,1)}, u32[]{:S(2)}) copy-start(bf16[2,3,64,512]{3,2,1,0:T(8,128)(2,1)} %get-tuple-element.27) | copy-start | bytes 1179652
  47.4 2.8 %copy-start.1 = (bf16[4,64,512]{2,1,0:T(8,128)(2,1)S(1)}, bf16[4,64,512]{2,1,0:T(8,128)(2,1)}, u32[]{:S(2)}) copy-start(bf16[4,64,512]{2,1,0:T(8,128)(2,1)} %feat.1) | copy-start | bytes 786436
  49.6 0.9 copy-start.10
  53.2 2.1 %copy-start = (bf16[4,64,512]{2,1,0:T(8,128)(2,1)}, bf16[4,64,512]{2,1,0:T(8,128)(2,1)S(1)}, u32[]{:S(2)}) copy-start(bf16[4,64,512]{2,1,0:T(8,128)(2,1)S(1)} %get-tuple-element.106.dconv) | copy-start | bytes 786436
  54.6 1.0 copy-start.11
  54.6 1.0 copy-start.12
  55.4 1.9 %copy-start.9 = (bf16[4,64,512]{2,1,0:T(8,128)(2,1)S(1)}, bf16[4,64,512]{2,1,0:T(8,128)(2,1)}, u32[]{:S(2)}) copy-start(bf16[4,64,512]{2,1,0:T(8,128)(2,1)} %get-tuple-element.21) | copy-start | bytes 786436
  62.6 37.3 %copy-start.13 = (f32[1,512]{1,0:T(1,128)S(1)}, f32[1,512]{1,0:T(1,128)}, u32[]{:S(2)}) copy-start(f32[1,512]{1,0:T(1,128)} %get-tuple-element.110) | copy-start | bytes 6148
  62.6 37.3 %copy-start.15 = (bf16[16,128,512]{2,1,0:T(8,128)(2,1)S(1)}, bf16[16,128,512]{2,1,0:T(8,128)(2,1)}, u32[]{:S(2)}) copy-start(bf16[16,128,512]{2,1,0:T(8,128)(2,1)} %get-tuple-element.24) | copy-start | bytes 6291460
  99.9 1.5 %copy-start.8 = (bf16[4,64,512]{2,1,0:T(8,128)(2,1)S(1)}, bf16[4,64,512]{2,1,0:T(8,128)(2,1)}, u32[]{:S(2)}) copy-start(bf16[4,64,512]{2,1,0:T(8,128)(2,1)} %get-tuple-element.133) | copy-start | bytes 786436
  99.9 2.2 %copy-start.7 = (f32[32,2048]{1,0:T(8,128)S(1)}, f32[32,2048]{1,0:T(8,128)}, u32[]{:S(2)}) copy-start(f32[32,2048]{1,0:T(8,128)} %get-tuple-element.134) | copy-start | bytes 786436
  99.9 2.9 %copy-start.6 = (f32[128,512]{1,0:T(8,128)S(1)}, f32[128,512]{1,0:T(8,128)}, u32[]{:S(2)}) copy-start(f32[128,512]{1,0:T(8,128)} %get-tuple-element.135) | copy-start | bytes 786436

commit v3 on v2

--- a/solution.py
+++ b/solution.py
@@ -113,6 +113,41 @@
                 moved = sources[part] if shift == 0 else pltpu.roll(sources[part], shift, 1)
                 total = jnp.where(spot == part, moved, total)
             wide[block * rows : (block + 1) * rows, group * LANES : (group + 1) * LANES] = total
+
+
+def pack(wide, packed, devices, own):
+    pieces = LANES // own
+    rows = packed.shape[1]
+    spot = lax.broadcasted_iota(jnp.int32, (rows, LANES), 1) // own
+    for group in range(devices // pieces):
+        sources = [
+            wide[block * rows : (block + 1) * rows, group * LANES : (group + 1) * LANES] for block in range(pieces)
+        ]
+        for part in range(pieces):
+            total = jnp.zeros((rows, LANES), jnp.float32)
+            for block in range(pieces):
+                shift = ((block - part) * own) % LANES
+                moved = sources[block] if shift == 0 else pltpu.roll(sources[block], shift, 1)
+                total = jnp.where(spot == block, moved, total)
+            packed[group * pieces + part] = total
+
+
+def tap_sums(wide_dconv, wide_feat, terms, first, height, width, scale):
+    chans = wide_feat.shape[2]
+
+    @pl.loop(0, chans // LANES)
+    def _(group):
+        lanes = pl.ds(pl.multiple_of(group * LANES, LANES), LANES)
+        for second in range(7):
+            begin = LEFT - HALO + second
+            total = jnp.zeros((width, LANES), jnp.float32)
+            for row in range(height):
+                total = total + (
+                    wide_dconv[HALO + row, LEFT : LEFT + width, lanes]
+                    * wide_feat[row + first, begin : begin + width, lanes]
+                )
+            tap = first * 7 + second
+            terms[tap : tap + 1, lanes] = jnp.sum(total, axis=0, keepdims=True) * scale
 
 
 def rows_at(step, most, height):
@@ -280,9 +315,9 @@
 
 
 def scatter_kernel(
-    ring, up, down, small, dconv, wide, cot,
+    ring, scale, up, down, rest, dconv, wide, cot, feat, feat_rim,
     own_up, own_down, own_small, grad_feat,
-    half_up, half_down, got_up, got_down, out_up, out_down, got_small, rim, wide_rows,
+    half_up, half_down, got_up, got_down, out_up, out_down, got_small, rim, wide_rows, wide_feat, terms, small,
     ring_out, ring_in, pair_out, pair_in, small_out, small_in, rim_out, rim_in,
 ):
     devices = ring.devices
@@ -335,10 +370,6 @@
     def small_copy(step):
         target = lax.rem(me + step, devices)
         return send(small.at[target], got_small.at[step], small_out.at[step], small_in.at[step], target)
-
-    @pl.loop(1, devices)
-    def _(step):
-        small_copy(step).start()
 
     def hop(flow, step):
         direction, which, _ = ring.flows[flow]
@@ -391,6 +422,19 @@
                 lower_rim().wait_recv()
 
             fill_rims(wide_rows, rim, height, width)
+            fill_middle(wide_feat, feat)
+            fill_rims(wide_feat, feat_rim, height, width)
+            terms[...] = rest[...]
+        for first in range(7):
+            if first * ring.most // 7 + 1 == step:
+                tap_sums(wide_rows, wide_feat, terms, first, height, width, scale)
+        if step == ring.most:
+            pack(terms, small, devices, terms.shape[1] // devices)
+
+            @pl.loop(1, devices)
+            def _(other):
+                small_copy(other).start()
+
         for row in rows_at(step, ring.most, height):
             spread(row)
 
@@ -466,21 +510,22 @@
     )(up, down, small, feat)
 
 
-def scatter(ring, up, down, small, dconv, wide, cot):
+def scatter(ring, scale, up, down, rest, dconv, wide, cot, feat, feat_rim):
     height, width, chans = dconv.shape
     devices, most, flows, chips = ring.devices, ring.most, len(ring.flows), ring.chips
     dma = pltpu.SemaphoreType.DMA
     block_up, block_down = up.shape[2:], down.shape[2:]
     kind = up.dtype
+    packed = (devices, rest.shape[0] * rest.shape[1] // devices // LANES, LANES)
     return pl.pallas_call(
-        functools.partial(scatter_kernel, ring),
+        functools.partial(scatter_kernel, ring, scale),
         out_shape=(
             jax.ShapeDtypeStruct(block_up, jnp.float32),
             jax.ShapeDtypeStruct(block_down, jnp.float32),
-            jax.ShapeDtypeStruct(small.shape[1:], jnp.float32),
+            jax.ShapeDtypeStruct(packed[1:], jnp.float32),
             jax.ShapeDtypeStruct(cot.shape, cot.dtype),
         ),
-        in_specs=[vmem()] * 6,
+        in_specs=[vmem()] * 8,
         out_specs=(vmem(),) * 4,
         scratch_shapes=[
             pltpu.VMEM((chips,) + block_up, kind),
@@ -489,9 +534,12 @@
             pltpu.VMEM((2, most) + block_down, kind),
             pltpu.VMEM((2, most) + block_up, kind),
             pltpu.VMEM((2, most) + block_down, kind),
-            pltpu.VMEM(small.shape, jnp.float32),
+            pltpu.VMEM(packed, jnp.float32),
             pltpu.VMEM((2, HALO, width, chans), dconv.dtype),
             pltpu.VMEM((height + 2 * HALO, width + 2 * LEFT, chans), jnp.float32),
+            pltpu.VMEM((height + 2 * HALO, width + 2 * LEFT, chans), jnp.float32),
+            pltpu.VMEM(rest.shape, jnp.float32),
+            pltpu.VMEM(packed, jnp.float32),
             dma((flows, most)), dma((flows, most)),
             dma((2, chips)), dma((2, chips)),
             dma((devices,)), dma((devices,)),
@@ -501,7 +549,7 @@
             collective_id=1, has_side_effects=True, vmem_limit_bytes=56 * 2**20
         ),
         name="scatter",
-    )(up, down, small, dconv, wide, cot)
+    )(up, down, rest, dconv, wide, cot, feat, feat_rim)
 
 
 def gelu_parts(value):
@@ -547,8 +595,6 @@
     down_full = all_down.reshape(units, chans)
     gain, bias_down = wide[taps + 1], wide[taps + 3]
     bias_up = wide[taps + 4 : taps + 4 + ratio].reshape(ratio, devices, own).transpose(1, 0, 2).reshape(units)
-    rimmed = jnp.concatenate([rim[0], features, rim[1]], axis=0)
-    padded = jnp.pad(rimmed.astype(jnp.float32), ((0, 0), (3, 3), (0, 0)))
     flat_norm = normal_out.reshape(cells, chans)
     flat_cot = cotangent.reshape(cells, chans)
     hidden = jnp.dot(flat_norm, up_full, preferred_element_type=jnp.float32) + bias_up
@@ -579,32 +625,29 @@
     )
     dconv = dconv.astype(jnp.bfloat16)
     dconv_wide = dconv.astype(jnp.float32)
-    tap_terms = []
-    for first in range(7):
-        for second in range(7):
-            tap_terms.append(
-                jnp.sum(dconv_wide * padded[first : first + height, second : second + width, :], axis=(0, 1))
-            )
     conv_bias_term = jnp.sum(dconv_wide, axis=(0, 1))
     terms = jnp.concatenate(
         [
-            jnp.stack(tap_terms + [conv_bias_term, gain_term, shift_term, down_bias_term], axis=0),
+            jnp.zeros((taps, chans), jnp.float32),
+            jnp.stack([conv_bias_term, gain_term, shift_term, down_bias_term], axis=0),
             up_bias_term.reshape(devices, ratio, own).transpose(1, 0, 2).reshape(ratio, chans),
         ],
         axis=0,
     ) * scale
     terms = jnp.pad(terms, ((0, filled - rows), (0, 0)))
-    terms = terms.reshape(filled, devices, own).transpose(1, 0, 2).reshape(devices, filled * own // LANES, LANES)
     grad_up, grad_down, own_terms, grad_features = scatter(
         ring,
+        scale,
         up_part.reshape(ring.chips, 2, chans // devices, units),
         down_part.reshape(ring.chips, 2, units // devices, chans),
         terms,
         dconv,
         wide,
         cotangent,
-    )
-    own_terms = own_terms.reshape(filled, own)
+        features,
+        rim,
+    )
+    own_terms = own_terms.reshape(filled // pieces, pieces, own).transpose(1, 0, 2).reshape(filled, own)
     return (
         block_out,
         grad_features,

time: 104 us -> 102 us (0.981)
  other arithmetic: 6.32 us -> 3.71 us
  matrix products: 12.3 us -> 9.84 us
  local copies, waits for them, and re-layouts: 12.1 us -> 14.4 us
  Pallas kernels: 71.9 us -> 73 us
    reduce_sum x3 -> x1, other arithmetic: 4.68 us -> 0.88 us  [per_device(): conv_bias_term = jnp.sum(dconv_wide, axis=(0, 1))]
    unnamed x40 -> x17, local copies, waits for them, and re-layouts: 3.96 us -> 7.45 us
    dot_general x1, matrix products: 2.18 us -> 0.91 us  [per_device(): lax.dot_general(dhidden, up_full, (((1,), (1,)), ((), ())), preferred_ele...]
    dot_general x1, matrix products: 3.25 us -> 2.03 us  [per_device(): lax.dot_general(flat_norm, dhidden, (((0,), (0,)), ((), ())), preferred_e...]
    pallas_call x1, Pallas kernels: 34.7 us -> 35.8 us  [scatter(): pl.pallas_call(functools.partial(scatter_kernel, ring, scale), out_shape=...]
where the time goes in v3:
time: 102 us
  Pallas kernels  73 us (72%)
  local copies, waits for them, and re-layouts  14.4 us (14%)
  matrix products  9.84 us (10%)
  other arithmetic  3.71 us (4%)
    pallas_call x1, Pallas kernels, gather(): pl.pallas_call(functools.partial(gather_kernel, ring, taps), out_shape=(j...  37.2 us
    pallas_call x1, Pallas kernels, scatter(): pl.pallas_call(functools.partial(scatter_kernel, ring, scale), out_shape=...  35.8 us
    unnamed x17, local copies, waits for them, and re-layouts  7.45 us
    dot_general x1, matrix products, per_device(): jnp.dot(flat_norm, up_full, preferred_element_type=jnp.float32) + bias_up  2.68 us
    dot_general x1, matrix products, per_device(): lax.dot_general(act, flat_cot, (((0,), (0,)), ((), ())), preferred_elemen...  2.1 us

profile of v3, /device:TPU:0, one launch (start us, length us, event | category | flops | bytes accessed | tf_op | source)
XLA Modules:
  0.0 101.7 jit_solution(12741853495257260039)
XLA Ops:
  0.6 0.7 reshape.80
  1.4 1.0 convert_reduce_fusion.1
  2.4 0.8 copy.28
  3.2 0.8 concatenate.6
  4.1 0.7 reshape.82.small
  4.7 37.2 %gather.1 = (bf16[16,32,2048]{2,1,0:T(8,128)(2,1)}, bf16[16,128,512]{2,1,0:T(8,128)(2,1)}, f32[64,512]{1,0:T(8,128)}, bf16[2,3,64,512]{3,2,1,0:T(8,128)(2,1)}, f...) custom-call(bf16[32,2048]{1,0:T(8,128)(2,1)} %up.1, bf16[128,512]{1,0:T(8,128)(2,1)} %down.1, ...), custom_call_target="tpu_custom_call" | custom-call | tf_op jit(solution)/shard_map/gather/pallas_call | solution.py:484
  41.9 1.0 reduce.1
  42.9 0.8 fusion.6
  43.7 0.8 slice.27
  44.5 0.1 reshape.85
  44.6 0.1 add.36
  44.7 0.0 copy-start.2
  44.7 0.0 copy-start.5
  44.7 2.7 %multiply_convert_fusion.2 = (bf16[256,2048]{1,0:T(8,128)(2,1)S(1)}, f32[256,2048]{1,0:T(8,128)S(1)}) fusion(f32[2048]{0:T(1024)S(1)} %add.36, bf16[256,512]{1,0:T(8,128)(2,1)} %bitcast.63, bf16[512,2048]{1,0:T(8,128)(2,1)} %bitcast.56), kind=kOutput, calls=%fused_computation.12 | convolution fusion | flops 540016640 | bytes 5513216 | tf_op jit(solution)/shard_map/dot_general | solution.py:600
  47.4 0.0 copy-done.2
  47.4 0.0 copy-done.5
  47.4 1.4 %convert_reduce_fusion = (f32[2048]{0:T(1024)S(1)}, bf16[256,2048]{1,0:T(8,128)(2,1)S(1)}) fusion(f32[256,2048]{1,0:T(8,128)S(1)} %get-tuple-element.55, bf16[2048,512]{1,0:T(8,128)(2,1)S(1)} %bitcast.82, bf16[256,512]{1,0:T(8,128)(2,1)S(1)} %bitcast.60), kind=kOutput, calls=%fused_computation.11 | convolution fusion | flops 543160320 | bytes 5513216 | tf_op jit(solution)/shard_map/dot_general | solution.py:609
  48.8 0.0 copy-start.1
  48.8 0.0 copy-start.3
  48.8 0.7 convolution_add_fusion.1
  49.6 0.8 copy-done.1
  50.4 0.1 copy-done.3
  50.5 0.0 copy-start
  50.5 0.9 multiply_reduce_fusion
  51.4 0.0 copy-done
  51.4 0.8 add_convert_fusion
  52.2 0.9 convert_reduce_fusion.2
  53.1 0.1 reshape.91
  53.2 0.1 reshape.92
  53.3 0.1 concatenate.7
  53.5 0.7 pad.9.rest
  54.1 0.0 copy-start.4
  54.1 2.1 %multiply_convert_fusion = bf16[2048,512]{1,0:T(8,128)(2,1)} fusion(bf16[256,2048]{1,0:T(8,128)(2,1)S(1)} %get-tuple-element.54, bf16[256,512]{1,0:T(8,128)(2,1)S(1)} %bitcast.61), kind=kOutput, calls=%fused_computation | convolution fusion | flops 538968064 | bytes 3407872 | tf_op jit(solution)/shard_map/dot_general | solution.py:607
  56.2 0.0 copy-done.4
  56.2 2.0 %multiply_convert_fusion.1 = bf16[512,2048]{1,0:T(8,128)(2,1)} fusion(bf16[256,512]{1,0:T(8,128)(2,1)S(1)} %bitcast.64, bf16[256,2048]{1,0:T(8,128)(2,1)S(1)} %get-tuple-element.58), kind=kOutput, calls=%fused_computation.1 | convolution fusion | flops 538968064 | bytes 3407872 | tf_op jit(solution)/shard_map/dot_general | solution.py:612
  58.3 35.8 %scatter.1 = (f32[32,2048]{1,0:T(8,128)}, f32[128,512]{1,0:T(8,128)}, f32[16,128]{1,0:T(8,128)}, bf16[4,64,512]{2,1,0:T(8,128)(2,1)}) custom-call(bf16[8,2,32,2048]{3,2,1,0:T(8,128)(2,1)} %bitcast.59, bf16[8,2,128,512]{3,2,1,0:T(8,128)(2,1)} %bitcast.58, f32[64,512]{1,0:T(8,128)} %pad.9.rest, bf16[4,64,512]{2,1,0:T(8,128)(2,1)} %get-tuple-element.47.dconv, ...), custom_call_target="tpu_custom_call" | custom-call | tf_op jit(solution)/shard_map/scatter/pallas_call | solution.py:520
  94.1 0.8 reshape.93
  94.9 0.6 reshape.95
  95.5 0.5 slice_bitcast_fusion
  96.0 0.7 copy.33
  96.7 1.7 %copy.39 = bf16[4,64,512]{2,1,0:T(8,128)(2,1)} copy(bf16[4,64,512]{2,1,0:T(8,128)(2,1)} %get-tuple-element.72) | data formatting | bytes 524288
  98.4 1.7 %copy.40 = f32[32,2048]{1,0:T(8,128)} copy(f32[32,2048]{1,0:T(8,128)} %get-tuple-element.73) | data formatting | bytes 524288
  100.0 1.7 %copy.41 = f32[128,512]{1,0:T(8,128)} copy(f32[128,512]{1,0:T(8,128)} %get-tuple-element.74) | data formatting | bytes 524288
  (10 shorter events, 0.1 us)
Async XLA Ops:
  44.7 2.7 %copy-start.2 = (bf16[4,64,512]{2,1,0:T(8,128)(2,1)S(1)}, bf16[4,64,512]{2,1,0:T(8,128)(2,1)}, u32[]{:S(2)}) copy-start(bf16[4,64,512]{2,1,0:T(8,128)(2,1)} %cot.1) | copy-start | bytes 786436
  44.7 2.7 %copy-start.5 = (bf16[16,128,512]{2,1,0:T(8,128)(2,1)S(1)}, bf16[16,128,512]{2,1,0:T(8,128)(2,1)}, u32[]{:S(2)}) copy-start(bf16[16,128,512]{2,1,0:T(8,128)(2,1)} %get-tuple-element.24) | copy-start | bytes 6291460
  48.8 1.6 %copy-start.1 = (bf16[16,32,2048]{2,1,0:T(8,128)(2,1)S(1)}, bf16[16,32,2048]{2,1,0:T(8,128)(2,1)}, u32[]{:S(2)}) copy-start(bf16[16,32,2048]{2,1,0:T(8,128)(2,1)} %get-tuple-element.22) | copy-start | bytes 6291460
  48.8 1.7 %copy-start.3 = (f32[4,64,512]{2,1,0:T(8,128)S(1)}, f32[4,64,512]{2,1,0:T(8,128)}, u32[]{:S(2)}) copy-start(f32[4,64,512]{2,1,0:T(8,128)} %get-tuple-element.26) | copy-start | bytes 1572868
  50.5 0.9 copy-start
  54.1 2.1 %copy-start.4 = (bf16[4,64,512]{2,1,0:T(8,128)(2,1)S(1)}, bf16[4,64,512]{2,1,0:T(8,128)(2,1)}, u32[]{:S(2)}) copy-start(bf16[4,64,512]{2,1,0:T(8,128)(2,1)} %get-tuple-element.21) | copy-start | bytes 786436
